TPU v7x, 256 devices: a whole 4x4x8 slice. The times are simulated.
256 devices in a mesh: row: 16 (over z_lo, y, core), col: 16 (over z_hi, x).
Axes of the slice: x: 4, y: 4, z: 8 (z_hi: 4, z_lo: 2; z = z_hi * 2 + z_lo), core: 2. Of those that a mesh axis runs over, the one named last changes fastest.
Arguments:
- state: float32 [3, 2048, 4096], P(None, 'row', 'col'), may hold values from -0.675 to 1.5, as said below
- row_count: int32 [16, 16], P('row', 'col'), may hold values from 0 to 64, as said below
- col_count: int32 [16, 16], P('row', 'col'), may hold values from 0 to 64, as said below
- patch_pos: int32 [16, 16, 2], P('row', 'col'), may hold values from 0 to 192, as said below
- patch_ext: int32 [16, 16, 2], P('row', 'col'), may hold values from 16 to 64, as said below
Outputs:
- richardson_error: float32 [1024, 2048], P('row', 'col')
- moved_state: float32 [3, 2048, 4096], P(None, 'row', 'col')
- refined_patch: float32 [3, 2048, 2048], P(None, 'row', 'col')
Inputs may be any that keep to these rules, and one draw needn't show every extreme that they name: `state`: depth lies in [0.5, 1.5]; the momenta are depth times a velocity of magnitude at most 0.45. `row_count`: some tile takes over exactly 64 rows and some none. `col_count`: some tile takes over exactly 64 columns and some none. `patch_pos`: component 0 is at most 64 and component 1 at most 192; both ends are reached. `patch_ext`: some tile is flagged over its whole patch.
All inputs are finite; a program needn't handle non-finite values.
Results may differ from a plain program's by a relative error of at most 0.0003.
Values sent between devices are 32-bit elements; how exact they have to be, the bound alone decides.
A program may use at most 128 MiB of HBM per device.

v0:
```python
import math

import jax
import jax.numpy as jnp
from jax import lax
from jax.sharding import PartitionSpec as P

SLAB = 64
PATCH = 64


GRAV = 1.0
RATIO = 0.1
ERR_SCALE = 10.0


def with_halo(value, sides, width):
    for axis, dim in sides:
        devices, length = (lax.axis_size(axis), value.shape[dim])
        up = [(i, (i + 1) % devices) for i in range(devices)]
        down = [(j, i) for i, j in up]
        last = lax.slice_in_dim(value, length - width, length, axis=dim)
        first = lax.slice_in_dim(value, 0, width, axis=dim)
        before = lax.ppermute(last, axis, up)
        after = lax.ppermute(first, axis, down)
        value = jnp.concatenate([before, value, after], axis=dim)
    return value


def shifted(value, axis, by):
    devices = lax.axis_size(axis)
    return lax.ppermute(value, axis, [(i, (i + by) % devices) for i in range(devices)])


def face_flux(left_vals, right_vals, normal):
    tangent = 3 - normal

    def physical(fields):
        depth = fields[0]
        velocity = fields[normal] / depth
        flux = [None, None, None]
        flux[0] = fields[normal]
        flux[normal] = fields[normal] * velocity + 0.5 * GRAV * depth * depth
        flux[tangent] = fields[tangent] * velocity
        return (flux, jnp.abs(velocity) + jnp.sqrt(GRAV * depth))

    flux_left, speed_left = physical(left_vals)
    flux_right, speed_right = physical(right_vals)
    speed = jnp.maximum(speed_left, speed_right)
    return [
        0.5 * (flux_left[comp] + flux_right[comp])
        - 0.5 * speed * (right_vals[comp] - left_vals[comp])
        for comp in range(3)
    ]


def rusanov_step(cells):
    fields = [cells[comp] for comp in range(3)]
    flux_row = face_flux([f[:-1, 1:-1] for f in fields], [f[1:, 1:-1] for f in fields], 1)
    flux_col = face_flux([f[1:-1, :-1] for f in fields], [f[1:-1, 1:] for f in fields], 2)
    result = [
        fields[comp][1:-1, 1:-1]
        - RATIO * (flux_row[comp][1:] - flux_row[comp][:-1])
        - RATIO * (flux_col[comp][:, 1:] - flux_col[comp][:, :-1])
        for comp in range(3)
    ]
    return jnp.stack(result)


def coarsen(cells):
    shaped = cells.reshape(cells.shape[0], cells.shape[1] // 2, 2, cells.shape[2] // 2, 2)
    return 0.25 * (
        shaped[:, :, 0, :, 0]
        + shaped[:, :, 1, :, 0]
        + shaped[:, :, 0, :, 1]
        + shaped[:, :, 1, :, 1]
    )


def richardson(fine_two, coarse_one):
    return ERR_SCALE * jnp.sum(jnp.abs(coarsen(fine_two) - coarse_one), axis=0)


def minmod(lower_diff, upper_diff):
    chosen = jnp.where(jnp.abs(lower_diff) < jnp.abs(upper_diff), lower_diff, upper_diff)
    return jnp.where(lower_diff * upper_diff > 0, chosen, 0.0)


def muscl_step(cells):
    fields = [cells[comp] for comp in range(3)]
    inner_rows = cells.shape[1] - 4
    inner_cols = cells.shape[2] - 4
    row_band = [f[:, 2:-2] for f in fields]
    deltas = [b[1:] - b[:-1] for b in row_band]
    slopes = [minmod(d[:-1], d[1:]) for d in deltas]
    left_vals = [
        row_band[c][1 : inner_rows + 2] + 0.5 * slopes[c][: inner_rows + 1] for c in range(3)
    ]
    right_vals = [
        row_band[c][2 : inner_rows + 3] - 0.5 * slopes[c][1 : inner_rows + 2] for c in range(3)
    ]
    flux_row = face_flux(left_vals, right_vals, 1)
    col_band = [f[2:-2, :] for f in fields]
    deltas = [b[:, 1:] - b[:, :-1] for b in col_band]
    slopes = [minmod(d[:, :-1], d[:, 1:]) for d in deltas]
    left_vals = [
        col_band[c][:, 1 : inner_cols + 2] + 0.5 * slopes[c][:, : inner_cols + 1] for c in range(3)
    ]
    right_vals = [
        col_band[c][:, 2 : inner_cols + 3] - 0.5 * slopes[c][:, 1 : inner_cols + 2]
        for c in range(3)
    ]
    flux_col = face_flux(left_vals, right_vals, 2)
    result = [
        fields[comp][2:-2, 2:-2]
        - RATIO * (flux_row[comp][1:] - flux_row[comp][:-1])
        - RATIO * (flux_col[comp][:, 1:] - flux_col[comp][:, :-1])
        for comp in range(3)
    ]
    return jnp.stack(result)


def by_blocks(step_fn, padded, rows_out, rim):
    block = math.gcd(rows_out, 16)
    count = rows_out // block

    def one_block(index):
        piece = lax.dynamic_slice_in_dim(padded, index * block, block + 2 * rim, padded.ndim - 2)
        return step_fn(piece)

    stacked = lax.map(one_block, jnp.arange(count, dtype=jnp.int32))
    stacked = jnp.moveaxis(stacked, 0, -3)
    shape = stacked.shape
    return stacked.reshape(shape[:-3] + (shape[-3] * shape[-2], shape[-1]))


def place_top(own_cells, slab_in, count_in):
    buffer = jnp.concatenate([slab_in, jnp.zeros_like(slab_in)], axis=1)
    aligned = lax.dynamic_slice_in_dim(buffer, SLAB - count_in, SLAB, 1)
    row_ids = lax.broadcasted_iota(jnp.int32, (1, SLAB, 1), 1)
    return jnp.where(row_ids < count_in, aligned, own_cells)


def place_cols(own_cells, slab_in, count_in):
    buffer = jnp.concatenate([slab_in, jnp.zeros_like(slab_in)], axis=2)
    aligned = lax.dynamic_slice_in_dim(buffer, SLAB - count_in, SLAB, 2)
    col_ids = lax.broadcasted_iota(jnp.int32, (1, 1, SLAB), 2)
    left_part = jnp.where(col_ids < count_in, aligned, own_cells[:, :, :SLAB])
    return jnp.concatenate([left_part, own_cells[:, :, SLAB:]], axis=2)


def refine_patch(padded, row_start, col_start, extent):
    zero_index = jnp.zeros((), jnp.int32)
    region = lax.dynamic_slice(
        padded, (zero_index, row_start, col_start), (3, PATCH + 4, PATCH + 4)
    )
    refined_cells = jnp.broadcast_to(
        region[:, :, None, :, None], (3, PATCH + 4, 2, PATCH + 4, 2)
    ).reshape(3, 2 * PATCH + 8, 2 * PATCH + 8)
    halfway = muscl_step(refined_cells)
    finished = muscl_step(halfway)
    row_ids = lax.broadcasted_iota(jnp.int32, (1, 2 * PATCH, 1), 1)
    col_ids = lax.broadcasted_iota(jnp.int32, (1, 1, 2 * PATCH), 2)
    inside = (row_ids < 2 * extent[0]) & (col_ids < 2 * extent[1])
    return jnp.where(inside, finished, 0.0)


def per_device(state, row_count, col_count, patch_pos, patch_ext):
    tile_rows = state.shape[1]
    tile_cols = state.shape[2]
    padded = with_halo(state, (("row", 1), ("col", 2)), 1)
    fine_one = by_blocks(rusanov_step, padded, tile_rows, 1)
    fine_rim = with_halo(fine_one, (("row", 1), ("col", 2)), 1)
    fine_two = by_blocks(rusanov_step, fine_rim, tile_rows, 1)
    coarse_rim = with_halo(coarsen(state), (("row", 1), ("col", 2)), 1)
    coarse_one = by_blocks(rusanov_step, coarse_rim, tile_rows // 2, 1)
    error_field = richardson(fine_two, coarse_one)
    upper_slab = shifted(state[:, tile_rows - SLAB :, :], "row", 1)
    top_rows = place_top(state[:, :SLAB, :], upper_slab, row_count[0, 0])
    row_moved = jnp.concatenate([top_rows, state[:, SLAB:, :]], axis=1)
    left_slab = shifted(row_moved[:, :, tile_cols - SLAB :], "col", 1)
    moved_state = place_cols(row_moved, left_slab, col_count[0, 0])
    padded_moved = with_halo(moved_state, (("row", 1), ("col", 2)), 2)
    patch_start = patch_pos[0, 0]
    refined = refine_patch(padded_moved, patch_start[0], patch_start[1], patch_ext[0, 0])
    return (error_field, moved_state, refined)


def solution(mesh):
    placed = (
        P(None, "row", "col"),
        P("row", "col"),
        P("row", "col"),
        P("row", "col", None),
        P("row", "col", None),
    )
    return jax.shard_map(
        per_device,
        mesh=mesh,
        in_specs=placed,
        out_specs=(P("row", "col"), P(None, "row", "col"), P(None, "row", "col")),
        check_vma=False,
    )
```

profile of v0, /device:TPU:57, one launch (start us, length us, event | category | flops | bytes accessed | tf_op | source)
XLA Modules:
  0.0 268.0 jit_solution(3986996809156444487)
XLA Ops:
  2.1 3.2 %collective-permute-start = (f32[3,1,256]{2,1,0:T(1,128)S(1)}, f32[3,1,256]{2,1,0:T(1,128)S(1)}, u32[]{:S(2)}, u32[]{:S(2)}) collective-permute-start(f32[3,1,256]{2,1,0:T(1,128)S(1)} %get-tuple-element.147), channel_id=1, source_target_pairs={{0,16},{16,32},{32,48},{48,64},{64,80},{80,96},{96,112},{112,128},... | collective-permute-start | bytes 9224 | tf_op jit(solution)/shard_map/ppermute | solution.py:24
  5.3 27.3 %reshape.134 = f32[3,64,2,128,2]{4,3,2,1,0:T(8,128)} reshape(f32[3,128,256]{2,1,0:T(8,128)} %param.11) | data formatting | bytes 786432 | tf_op jit(solution)/shard_map/reshape | solution.py:71
  32.6 19.6 %fusion.79 = f32[3,64,128]{2,1,0:T(8,128)S(1)} fusion(f32[3,64,2,128,2]{4,3,2,1,0:T(8,128)} %reshape.134), kind=kLoop, calls=%fused_computation.152 | loop fusion | flops 98304 | bytes 491520 | tf_op jit(solution)/shard_map/mul | solution.py:72
  52.3 3.8 %collective-permute-start.8 = (f32[3,1,128]{2,1,0:T(1,128)S(1)}, f32[3,1,128]{2,1,0:T(1,128)S(1)}, u32[]{:S(2)}, u32[]{:S(2)}) collective-permute-start(f32[3,1,128]{2,1,0:T(1,128)S(1)} %get-tuple-element.157), channel_id=1, source_target_pairs={{0,16},{16,32},{32,48},{48,64},{64,80},{80,96},{96,112},{112,128},... | collective-permute-start | bytes 4616 | tf_op jit(solution)/shard_map/ppermute | solution.py:24
  64.0 7.4 %collective-permute-start.3 = (f32[3,130,1]{2,1,0:T(8,128)S(1)}, f32[3,130,1]{2,1,0:T(8,128)S(1)}, u32[]{:S(2)}, u32[]{:S(2)}) collective-permute-start(f32[3,130,1]{2,1,0:T(8,128)S(1)} %get-tuple-element.144), channel_id=1, source_target_pairs={{1,0},{2,1},{3,2},{4,3},{5,4},{6,5},{7,6},{8,7},{9,8},{10,9},{11,1... | collective-permute-start | bytes 4688 | tf_op jit(solution)/shard_map/ppermute | solution.py:25
  71.5 5.8 %collective-permute-start.11 = (f32[3,66,1]{2,1,0:T(8,128)S(1)}, f32[3,66,1]{2,1,0:T(8,128)S(1)}, u32[]{:S(2)}, u32[]{:S(2)}) collective-permute-start(f32[3,66,1]{2,1,0:T(8,128)S(1)} %get-tuple-element.156), channel_id=1, source_target_pairs={{1,0},{2,1},{3,2},{4,3},{5,4},{6,5},{7,6},{8,7},{9,8},{10,9},{11,1... | collective-permute-start | bytes 2384 | tf_op jit(solution)/shard_map/ppermute | solution.py:25
  77.5 2.2 collective-permute-done.3
  79.7 7.1 %collective-permute-done.2 = f32[3,130,1]{2,1,0:T(8,128)S(1)} collective-permute-done((f32[3,130,1]{2,1,0:T(8,128)S(1)}, f32[3,130,1]{2,1,0:T(8,128)S(1)}, u32[]{:S(2)}, u32[]{:S(2)}) %collective-permute-start.2) | collective-permute-done | bytes 1592 | tf_op jit(solution)/shard_map/ppermute | solution.py:24
  87.2 14.3 %while.30 = (s32[]{:T(128)}, f32[8,3,16,256]{3,2,1,0:T(8,128)S(1)}, s32[8]{0:T(128)S(1)}, f32[3,130,258]{2,1,0:T(8,128)S(1)}, s32[]{:T(128)}, /*index=5*/s32[]{:T(128)}, s32[]{}, s32[1]{0:T(128)}, s32[]{:T(128)}, s32[]{}) while((s32[]{:T(128)}, f32[8,3,16,256]{3,2,1,0:T(8,128)S(1)}, s32[8]{0:T(128)S(1)}, f32[3,130,258]{2,1,0:T(8,128)S(1)}, ...), condition=%wide.region_1.2_spmd, body=%wide.region_0.1_spmd.sunk | while | flops 377624 | bytes 809583 | solution.py:131
  101.5 1.6 collective-permute-start.5
  103.1 2.3 collective-permute-start.4
  108.4 6.5 %while.32 = (s32[]{:T(128)}, f32[4,3,16,128]{3,2,0,1:T(8,128)S(1)}, s32[4]{0:T(128)S(1)}, f32[3,66,130]{2,1,0:T(8,128)S(1)}, s32[]{:T(128)}, /*index=5*/s32[]{:T(128)}, s32[]{}, s32[1]{0:T(128)}, s32[]{:T(128)}, s32[]{}) while((s32[]{:T(128)}, f32[4,3,16,128]{3,2,0,1:T(8,128)S(1)}, s32[4]{0:T(128)S(1)}, f32[3,66,130]{2,1,0:T(8,128)S(1)}, ...), condition=%wide.region_5.6_spmd, body=%wide.region_4.5_spmd.sunk | while | flops 189080 | bytes 405615 | solution.py:131
  115.0 6.2 %collective-permute-done.6 = f32[3,130,1]{2,1,0:T(8,128)S(1)} collective-permute-done((f32[3,130,1]{2,1,0:T(8,128)S(1)}, f32[3,130,1]{2,1,0:T(8,128)S(1)}, u32[]{:S(2)}, u32[]{:S(2)}) %collective-permute-start.6) | collective-permute-done | bytes 1592 | tf_op jit(solution)/shard_map/ppermute | solution.py:24
  121.5 13.6 %while.31 = (s32[]{:T(128)}, f32[8,3,16,256]{3,2,1,0:T(8,128)S(1)}, s32[8]{0:T(128)S(1)}, f32[3,130,258]{2,1,0:T(8,128)S(1)}, s32[]{:T(128)}, /*index=5*/s32[]{:T(128)}, s32[]{}, s32[1]{0:T(128)}, s32[]{:T(128)}, s32[]{}) while((s32[]{:T(128)}, f32[8,3,16,256]{3,2,1,0:T(8,128)S(1)}, s32[8]{0:T(128)S(1)}, f32[3,130,258]{2,1,0:T(8,128)S(1)}, ...), condition=%wide.region_3.4_spmd, body=%wide.region_2.3_spmd.sunk | while | flops 377624 | bytes 809583 | solution.py:131
  135.1 26.6 %reshape_reshape.3 = f32[3,64,2,128,2]{4,3,2,1,0:T(8,128)} reshape(f32[3,8,16,256]{3,2,1,0:T(8,128)S(1)} %copy.13) | data formatting | bytes 786432 | tf_op jit(solution)/shard_map/reshape;reshape | solution.py:71
  161.7 19.5 %fusion.81 = f32[3,64,128]{2,1,0:T(8,128)S(1)} fusion(f32[3,64,2,128,2]{4,3,2,1,0:T(8,128)} %reshape_reshape.3), kind=kLoop, calls=%fused_computation.157 | loop fusion | flops 98304 | bytes 491520 | tf_op jit(solution)/shard_map/mul | solution.py:72
  181.7 12.9 %collective-permute-done.13 = f32[3,128,64]{2,1,0:T(8,128)S(1)} collective-permute-done((f32[3,128,64]{2,1,0:T(8,128)S(1)}, f32[3,128,64]{2,1,0:T(8,128)S(1)}, u32[]{:S(2)}, u32[]{:S(2)}) %collective-permute-start.13) | collective-permute-done | bytes 98336 | tf_op jit(solution)/shard_map/ppermute | solution.py:32
  195.4 13.6 %collective-permute-start.14 = (f32[3,2,256]{2,1,0:T(2,128)S(1)}, f32[3,2,256]{2,1,0:T(2,128)S(1)}, u32[]{:S(2)}, u32[]{:S(2)}) collective-permute-start(f32[3,2,256]{2,1,0:T(2,128)S(1)} %get-tuple-element.129), channel_id=1, source_target_pairs={{0,16},{16,32},{32,48},{48,64},{64,80},{80,96},{96,112},{112,128},... | collective-permute-start | bytes 18440 | tf_op jit(solution)/shard_map/ppermute | solution.py:24
  210.2 5.7 %collective-permute-start.17 = (f32[3,132,2]{2,1,0:T(8,128)S(1)}, f32[3,132,2]{2,1,0:T(8,128)S(1)}, u32[]{:S(2)}, u32[]{:S(2)}) collective-permute-start(f32[3,132,2]{2,1,0:T(8,128)S(1)} %get-tuple-element.139), channel_id=1, source_target_pairs={{1,0},{2,1},{3,2},{4,3},{5,4},{6,5},{7,6},{8,7},{9,8},{10,9},{11,1... | collective-permute-start | bytes 9512 | tf_op jit(solution)/shard_map/ppermute | solution.py:25
  216.8 6.7 %collective-permute-done.16 = f32[3,132,2]{2,1,0:T(8,128)S(1)} collective-permute-done((f32[3,132,2]{2,1,0:T(8,128)S(1)}, f32[3,132,2]{2,1,0:T(8,128)S(1)}, u32[]{:S(2)}, u32[]{:S(2)}) %collective-permute-start.16) | collective-permute-done | bytes 3200 | tf_op jit(solution)/shard_map/ppermute | solution.py:24
  223.8 2.7 broadcast_in_dim.96
  226.4 3.6 %broadcast_in_dim.97 = f32[132,136]{1,0:T(8,128)S(1)} reshape(f32[66,2,68,2]{3,2,1,0:T(8,128)} %broadcast_in_dim.96) | data formatting | bytes 143616 | tf_op jit(solution)/shard_map/broadcast_in_dim | solution.py:157
  230.3 2.7 broadcast_in_dim.98
  232.9 3.6 %broadcast_in_dim.99 = f32[132,136]{1,0:T(8,128)S(1)} reshape(f32[66,2,68,2]{3,2,1,0:T(8,128)} %broadcast_in_dim.98) | data formatting | bytes 143616 | tf_op jit(solution)/shard_map/broadcast_in_dim | solution.py:157
  236.7 2.7 %broadcast_in_dim.102 = f32[68,2,68,2]{3,2,1,0:T(8,128)} broadcast(f32[68,68]{1,0:T(8,128)S(1)} %get-tuple-element.154), dimensions={0,2} | broadcast | bytes 92480 | tf_op jit(solution)/shard_map/broadcast_in_dim | solution.py:157
  239.4 3.6 %broadcast_in_dim.103 = f32[136,136]{1,0:T(8,128)S(1)} reshape(f32[68,2,68,2]{3,2,1,0:T(8,128)} %broadcast_in_dim.102) | data formatting | bytes 147968 | tf_op jit(solution)/shard_map/broadcast_in_dim | solution.py:157
  243.3 2.7 %broadcast_in_dim.94 = f32[68,2,68,2]{3,2,1,0:T(8,128)} broadcast(f32[68,68]{1,0:T(8,128)S(1)} %get-tuple-element.153), dimensions={0,2} | broadcast | bytes 92480 | tf_op jit(solution)/shard_map/broadcast_in_dim | solution.py:157
  246.0 3.6 %broadcast_in_dim.95 = f32[136,136]{1,0:T(8,128)S(1)} reshape(f32[68,2,68,2]{3,2,1,0:T(8,128)} %broadcast_in_dim.94) | data formatting | bytes 147968 | tf_op jit(solution)/shard_map/broadcast_in_dim | solution.py:157
  249.8 2.7 %broadcast_in_dim.92 = f32[68,2,68,2]{3,2,1,0:T(8,128)} broadcast(f32[68,68]{1,0:T(8,128)S(1)} %get-tuple-element.152), dimensions={0,2} | broadcast | bytes 92480 | tf_op jit(solution)/shard_map/broadcast_in_dim | solution.py:157
  252.5 3.6 %broadcast_in_dim.93 = f32[136,136]{1,0:T(8,128)S(1)} reshape(f32[68,2,68,2]{3,2,1,0:T(8,128)} %broadcast_in_dim.92) | data formatting | bytes 147968 | tf_op jit(solution)/shard_map/broadcast_in_dim | solution.py:157
  258.0 2.7 broadcast_in_dim.100
  260.7 3.6 %broadcast_in_dim.101 = f32[132,136]{1,0:T(8,128)S(1)} reshape(f32[66,2,68,2]{3,2,1,0:T(8,128)} %broadcast_in_dim.100) | data formatting | bytes 143616 | tf_op jit(solution)/shard_map/broadcast_in_dim | solution.py:157
  (247 shorter events, 37.3 us)
Async XLA Ops:
  1.4 62.4 %collective-permute-start.1 = (f32[3,1,256]{2,1,0:T(1,128)S(1)}, f32[3,1,256]{2,1,0:T(1,128)S(1)}, u32[]{:S(2)}, u32[]{:S(2)}) collective-permute-start(f32[3,1,256]{2,1,0:T(1,128)S(1)} %get-tuple-element.148), channel_id=1, source_target_pairs={{16,0},{32,16},{48,32},{64,48},{80,64},{96,80},{112,96},{128,112},... | collective-permute-start | bytes 9224 | tf_op jit(solution)/shard_map/ppermute | solution.py:25
  2.1 61.7 %collective-permute-start = (f32[3,1,256]{2,1,0:T(1,128)S(1)}, f32[3,1,256]{2,1,0:T(1,128)S(1)}, u32[]{:S(2)}, u32[]{:S(2)}) collective-permute-start(f32[3,1,256]{2,1,0:T(1,128)S(1)} %get-tuple-element.147), channel_id=1, source_target_pairs={{0,16},{16,32},{32,48},{48,64},{64,80},{80,96},{96,112},{112,128},... | collective-permute-start | bytes 9224 | tf_op jit(solution)/shard_map/ppermute | solution.py:24
  32.6 23.6 %copy-start = (f32[3,128,256]{2,1,0:T(8,128)S(1)}, f32[3,128,256]{2,1,0:T(8,128)}, u32[]{:S(2)}) copy-start(f32[3,128,256]{2,1,0:T(8,128)} %param.11) | copy-start | bytes 1179652
  32.6 25.0 %copy-start.1 = (s32[1,1,2]{2,1,0:T(1,128)S(1)}, s32[1,1,2]{2,1,0:T(1,128)}, u32[]{:S(2)}) copy-start(s32[1,1,2]{2,1,0:T(1,128)} %param.14) | copy-start | bytes 28
  32.6 25.6 %copy-start.2 = (s32[1,1,2]{2,1,0:T(1,128)S(1)}, s32[1,1,2]{2,1,0:T(1,128)}, u32[]{:S(2)}) copy-start(s32[1,1,2]{2,1,0:T(1,128)} %param.15) | copy-start | bytes 28
  52.2 11.6 %collective-permute-start.9 = (f32[3,1,128]{2,1,0:T(1,128)S(1)}, f32[3,1,128]{2,1,0:T(1,128)S(1)}, u32[]{:S(2)}, u32[]{:S(2)}) collective-permute-start(f32[3,1,128]{2,1,0:T(1,128)S(1)} %get-tuple-element.158), channel_id=1, source_target_pairs={{16,0},{32,16},{48,32},{64,48},{80,64},{96,80},{112,96},{128,112},... | collective-permute-start | bytes 4616 | tf_op jit(solution)/shard_map/ppermute | solution.py:25
  52.3 11.5 %collective-permute-start.8 = (f32[3,1,128]{2,1,0:T(1,128)S(1)}, f32[3,1,128]{2,1,0:T(1,128)S(1)}, u32[]{:S(2)}, u32[]{:S(2)}) collective-permute-start(f32[3,1,128]{2,1,0:T(1,128)S(1)} %get-tuple-element.157), channel_id=1, source_target_pairs={{0,16},{16,32},{32,48},{48,64},{64,80},{80,96},{96,112},{112,128},... | collective-permute-start | bytes 4616 | tf_op jit(solution)/shard_map/ppermute | solution.py:24
  56.1 125.1 %collective-permute-start.12 = (f32[3,64,256]{2,1,0:T(8,128)S(1)}, f32[3,64,256]{2,1,0:T(8,128)S(1)}, u32[]{:S(2)}, u32[]{:S(2)}) collective-permute-start(f32[3,64,256]{2,1,0:T(8,128)S(1)} %slice.870), channel_id=1, source_target_pairs={{0,16},{16,32},{32,48},{48,64},{64,80},{80,96},{96,112},{112,128},... | collective-permute-start | bytes 589832 | tf_op jit(solution)/shard_map/ppermute | solution.py:32
  64.0 15.7 %collective-permute-start.3 = (f32[3,130,1]{2,1,0:T(8,128)S(1)}, f32[3,130,1]{2,1,0:T(8,128)S(1)}, u32[]{:S(2)}, u32[]{:S(2)}) collective-permute-start(f32[3,130,1]{2,1,0:T(8,128)S(1)} %get-tuple-element.144), channel_id=1, source_target_pairs={{1,0},{2,1},{3,2},{4,3},{5,4},{6,5},{7,6},{8,7},{9,8},{10,9},{11,1... | collective-permute-start | bytes 4688 | tf_op jit(solution)/shard_map/ppermute | solution.py:25
  71.4 15.4 %collective-permute-start.2 = (f32[3,130,1]{2,1,0:T(8,128)S(1)}, f32[3,130,1]{2,1,0:T(8,128)S(1)}, u32[]{:S(2)}, u32[]{:S(2)}) collective-permute-start(f32[3,130,1]{2,1,0:T(8,128)S(1)} %get-tuple-element.143), channel_id=1, source_target_pairs={{0,1},{1,2},{2,3},{3,4},{4,5},{5,6},{6,7},{7,8},{8,9},{9,10},{10,1... | collective-permute-start | bytes 4688 | tf_op jit(solution)/shard_map/ppermute | solution.py:24
  71.5 34.0 %collective-permute-start.11 = (f32[3,66,1]{2,1,0:T(8,128)S(1)}, f32[3,66,1]{2,1,0:T(8,128)S(1)}, u32[]{:S(2)}, u32[]{:S(2)}) collective-permute-start(f32[3,66,1]{2,1,0:T(8,128)S(1)} %get-tuple-element.156), channel_id=1, source_target_pairs={{1,0},{2,1},{3,2},{4,3},{5,4},{6,5},{7,6},{8,7},{9,8},{10,9},{11,1... | collective-permute-start | bytes 2384 | tf_op jit(solution)/shard_map/ppermute | solution.py:25
  77.2 28.2 %collective-permute-start.10 = (f32[3,66,1]{2,1,0:T(8,128)S(1)}, f32[3,66,1]{2,1,0:T(8,128)S(1)}, u32[]{:S(2)}, u32[]{:S(2)}) collective-permute-start(f32[3,66,1]{2,1,0:T(8,128)S(1)} %get-tuple-element.155), channel_id=1, source_target_pairs={{0,1},{1,2},{2,3},{3,4},{4,5},{5,6},{6,7},{7,8},{8,9},{9,10},{10,1... | collective-permute-start | bytes 2384 | tf_op jit(solution)/shard_map/ppermute | solution.py:24
  101.5 5.2 %collective-permute-start.5 = (f32[3,1,256]{2,1,0:T(1,128)S(1)}, f32[3,1,256]{2,1,0:T(1,128)S(1)}, u32[]{:S(2)}, u32[]{:S(2)}) collective-permute-start(f32[3,1,256]{2,1,0:T(1,128)S(1)} %get-tuple-element.146), channel_id=1, source_target_pairs={{16,0},{32,16},{48,32},{64,48},{80,64},{96,80},{112,96},{128,112},... | collective-permute-start | bytes 9224 | tf_op jit(solution)/shard_map/ppermute | solution.py:25
  103.1 3.6 %collective-permute-start.4 = (f32[3,1,256]{2,1,0:T(1,128)S(1)}, f32[3,1,256]{2,1,0:T(1,128)S(1)}, u32[]{:S(2)}, u32[]{:S(2)}) collective-permute-start(f32[3,1,256]{2,1,0:T(1,128)S(1)} %get-tuple-element.145), channel_id=1, source_target_pairs={{0,16},{16,32},{32,48},{48,64},{64,80},{80,96},{96,112},{112,128},... | collective-permute-start | bytes 9224 | tf_op jit(solution)/shard_map/ppermute | solution.py:24
  106.9 8.1 %collective-permute-start.7 = (f32[3,130,1]{2,1,0:T(8,128)S(1)}, f32[3,130,1]{2,1,0:T(8,128)S(1)}, u32[]{:S(2)}, u32[]{:S(2)}) collective-permute-start(f32[3,130,1]{2,1,0:T(8,128)S(1)} %get-tuple-element.142), channel_id=1, source_target_pairs={{1,0},{2,1},{3,2},{4,3},{5,4},{6,5},{7,6},{8,7},{9,8},{10,9},{11,1... | collective-permute-start | bytes 4688 | tf_op jit(solution)/shard_map/ppermute | solution.py:25
  108.0 13.2 %collective-permute-start.6 = (f32[3,130,1]{2,1,0:T(8,128)S(1)}, f32[3,130,1]{2,1,0:T(8,128)S(1)}, u32[]{:S(2)}, u32[]{:S(2)}) collective-permute-start(f32[3,130,1]{2,1,0:T(8,128)S(1)} %get-tuple-element.141), channel_id=1, source_target_pairs={{0,1},{1,2},{2,3},{3,4},{4,5},{5,6},{6,7},{7,8},{8,9},{9,10},{10,1... | collective-permute-start | bytes 4688 | tf_op jit(solution)/shard_map/ppermute | solution.py:24
  181.4 13.2 %collective-permute-start.13 = (f32[3,128,64]{2,1,0:T(8,128)S(1)}, f32[3,128,64]{2,1,0:T(8,128)S(1)}, u32[]{:S(2)}, u32[]{:S(2)}) collective-permute-start(f32[3,128,64]{2,1,0:T(8,128)S(1)} %fusion.85), channel_id=1, source_target_pairs={{0,1},{1,2},{2,3},{3,4},{4,5},{5,6},{6,7},{7,8},{8,9},{9,10},{10,1... | collective-permute-start | bytes 294920 | tf_op jit(solution)/shard_map/ppermute | solution.py:32
  194.8 14.8 %collective-permute-start.15 = (f32[3,2,256]{2,1,0:T(2,128)S(1)}, f32[3,2,256]{2,1,0:T(2,128)S(1)}, u32[]{:S(2)}, u32[]{:S(2)}) collective-permute-start(f32[3,2,256]{2,1,0:T(2,128)S(1)} %get-tuple-element.130), channel_id=1, source_target_pairs={{16,0},{32,16},{48,32},{64,48},{80,64},{96,80},{112,96},{128,112},... | collective-permute-start | bytes 18440 | tf_op jit(solution)/shard_map/ppermute | solution.py:25
  195.4 14.4 %collective-permute-start.14 = (f32[3,2,256]{2,1,0:T(2,128)S(1)}, f32[3,2,256]{2,1,0:T(2,128)S(1)}, u32[]{:S(2)}, u32[]{:S(2)}) collective-permute-start(f32[3,2,256]{2,1,0:T(2,128)S(1)} %get-tuple-element.129), channel_id=1, source_target_pairs={{0,16},{16,32},{32,48},{48,64},{64,80},{80,96},{96,112},{112,128},... | collective-permute-start | bytes 18440 | tf_op jit(solution)/shard_map/ppermute | solution.py:24
  210.1 13.3 %collective-permute-start.16 = (f32[3,132,2]{2,1,0:T(8,128)S(1)}, f32[3,132,2]{2,1,0:T(8,128)S(1)}, u32[]{:S(2)}, u32[]{:S(2)}) collective-permute-start(f32[3,132,2]{2,1,0:T(8,128)S(1)} %get-tuple-element.140), channel_id=1, source_target_pairs={{0,1},{1,2},{2,3},{3,4},{4,5},{5,6},{6,7},{7,8},{8,9},{9,10},{10,1... | collective-permute-start | bytes 9512 | tf_op jit(solution)/shard_map/ppermute | solution.py:24
  210.2 13.2 %collective-permute-start.17 = (f32[3,132,2]{2,1,0:T(8,128)S(1)}, f32[3,132,2]{2,1,0:T(8,128)S(1)}, u32[]{:S(2)}, u32[]{:S(2)}) collective-permute-start(f32[3,132,2]{2,1,0:T(8,128)S(1)} %get-tuple-element.139), channel_id=1, source_target_pairs={{1,0},{2,1},{3,2},{4,3},{5,4},{6,5},{7,6},{8,7},{9,8},{10,9},{11,1... | collective-permute-start | bytes 9512 | tf_op jit(solution)/shard_map/ppermute | solution.py:25
where the time goes:
time: 272 us; the launch traced here: 268 us
  local copies, waits for them, and re-layouts  107 us (39%)
  other arithmetic  56.4 us (21%)
  starting transfers between devices  46.8 us (17%)
  waiting for transfers between devices  36.4 us (13%)
  loops' own time  14 us (5%)
  between operations  7.64 us (3%)
    mul x2, other arithmetic, coarsen(): 0.25 * (shaped[:, :, 0, :, 0] + shaped[:, :, 1, :, 0] + shaped[:, :, 0, :...  39.1 us
    broadcast_in_dim x12, local copies, waits for them, and re-layouts, refine_patch(): jnp.broadcast_to(region[:, :, None, :, None], (3, PATCH + 4, 2, PATCH + 4...  37.7 us
    reshape x1, local copies, waits for them, and re-layouts, coarsen(): cells.reshape(cells.shape[0], cells.shape[1] // 2, 2, cells.shape[2] // 2...  27.3 us
    another operation x1, local copies, waits for them, and re-layouts, coarsen(): cells.reshape(cells.shape[0], cells.shape[1] // 2, 2, cells.shape[2] // 2...  26.6 us
    ppermute x8, starting transfers between devices, with_halo(): before = lax.ppermute(last, axis, up)  23.7 us
    ppermute x8, starting transfers between devices, with_halo(): after = lax.ppermute(first, axis, down)  22.9 us
    ppermute x8, waiting for transfers between devices, with_halo(): before = lax.ppermute(last, axis, up)  20.1 us
    another operation x3, loops' own time, by_blocks(): stacked = lax.map(one_block, jnp.arange(count, dtype=jnp.int32))  14 us
  transfers between devices with their start and end apart: 18, of which 7 were waited for; matrix products, arithmetic and copies ran while one was open for 44% of the time, Pallas kernels for 0%

commit v1 on v0

v1 whole, which is shorter than its diff:
```python
import functools

import jax
import jax.numpy as jnp
from jax import lax
from jax.experimental import pallas as pl
from jax.experimental.pallas import tpu as pltpu
from jax.sharding import PartitionSpec as P

MESH = pl.DeviceIdType.MESH
F32 = jnp.float32
SLAB = 64
HALF = 0.05
BASE = 64
ROWS = 208
N_MSG = 18


def chunk(start, size=8):
    return pl.ds(start, size)


def lanes(shape=(8, 128)):
    return lax.broadcasted_iota(jnp.int32, shape, 1)


def roll(x, by):
    return pltpu.roll(x, by % x.shape[1] if isinstance(by, int) else by, 1)


def speeds(h, m1, m2):
    return m1 / h, m2 / h, jnp.sqrt(h)


def side(u, vel, normal):
    h, m1, m2 = u
    v1, v2, wave = vel
    pressure = 0.5 * h * h
    if normal == 1:
        return u, (m1, m1 * v1 + pressure, m2 * v1), jnp.abs(v1) + wave
    return u, (m2, m1 * v2, m2 * v2 + pressure), jnp.abs(v2) + wave


def face(lower, upper):
    speed = jnp.maximum(lower[2], upper[2])
    return [
        (lower[1][c] + upper[1][c]) - speed * (upper[0][c] - lower[0][c])
        for c in range(3)
    ]


def minmod(a, b):
    chosen = jnp.where(jnp.abs(a) < jnp.abs(b), a, b)
    return jnp.where(a * b > 0, chosen, 0.0)


def from_lower(xs, lane):
    rolled = [roll(x, 1) for x in xs]
    return [jnp.where(lane == 0, rolled[g - 1], rolled[g]) for g in range(len(xs))]


def from_upper(xs, lane):
    rolled = [roll(x, 127) for x in xs]
    return [
        jnp.where(lane == 127, rolled[(g + 1) % len(xs)], rolled[g])
        for g in range(len(xs))
    ]


def speed_pass(src, vel, groups, first, last):
    def body(i, carry):
        at = chunk(pl.multiple_of(i * 8, 8))
        for g in range(groups):
            for k, value in enumerate(speeds(*(src[c, g, at, :] for c in range(3)))):
                vel[k, g, at, :] = value
        return carry

    lax.fori_loop(first, last, body, 0)


def step_pass(src, vel, dst, groups, keep, first, last):
    lane = lanes()

    def body(i, carry):
        row = pl.multiple_of(i * 8, 8)

        def load(shift, g, normal):
            at = chunk(row + shift)
            return side(
                [src[c, g, at, :] for c in range(3)],
                [vel[c, g, at, :] for c in range(3)],
                normal,
            )

        along = [load(0, g, 2) for g in range(groups)]
        flat = [[*s[0], s[1][0], s[1][1], s[1][2], s[2]] for s in along]
        shifted = [
            from_lower([flat[g][k] for g in range(groups)], lane)
            for k in (0, 1, 2, 4, 5, 6)
        ]
        low = []
        for g in range(groups):
            u = [shifted[k][g] for k in range(3)]
            lower = (u, (u[2], shifted[3][g], shifted[4][g]), shifted[5][g])
            low.append(face(lower, along[g]))
        high = [from_upper([low[g][c] for g in range(groups)], lane) for c in range(3)]
        for g in range(keep):
            here = load(0, g, 1)
            down = face(load(-1, g, 1), here)
            up = face(here, load(1, g, 1))
            for c in range(3):
                change = (up[c] - down[c]) + (high[c][g] - low[g][c])
                dst[c, g, chunk(row), :] = here[0][c] - HALF * change
        return carry

    lax.fori_loop(first, last, body, 0)


def coarse_rows(src, row, groups, c):
    lane = lanes()
    even = lax.rem(2 * lane, 128)
    out = []
    for g in range(groups):
        pair = src[c, g, pl.ds(row, 8, stride=2), :] + src[c, g, pl.ds(row + 1, 8, stride=2), :]
        pair = pair + roll(pair, 127)
        out.append(jnp.take_along_axis(pair, even, axis=1, mode="promise_in_bounds"))
    return [0.25 * jnp.where(lane < 64, out[0], out[1])] + [0.25 * x for x in out[2:]]


def exchange_kernel(
    n_row, n_col, state, row_count, col_count,
    st, lslab, ulslab, dlc, cnt, err,
    rpack, lpack, rslab, drslab, cnt_s, lr, rl, url, ulc, drc,
    vel, fine1, fine2, cgrid, cvel, cone,
    local_sem, send_sem, recv_sem,
):
    me_r, me_c = lax.axis_index("row"), lax.axis_index("col")

    def device(dr, dc):
        return (lax.rem(me_r + (dr + n_row), n_row), lax.rem(me_c + (dc + n_col), n_col))

    loads = [
        pltpu.make_async_copy(
            state.at[:, :, pl.ds(128 * g, 128)], st.at[:, g, pl.ds(BASE, 128), :], local_sem.at[g]
        )
        for g in range(2)
    ]
    loads[1].start()
    loads[0].start()
    barrier = pltpu.get_barrier_semaphore()
    around = [(a, b) for a in (-1, 0, 1) for b in (-1, 0, 1) if (a, b) != (0, 0)]
    for a, b in around:
        pl.semaphore_signal(barrier, inc=1, device_id=device(a, b), device_id_type=MESH)

    lane = lanes()
    lane1 = lanes((1, 128))
    cnt_s[...] = jnp.where(lane1 == 0, row_count[0, 0], col_count[0, 0])
    loads[1].wait()
    loads[0].wait()
    for c in range(3):
        right = left = None
        for k in range(16):
            at = chunk(BASE + 8 * k)
            mine = (lane >= 8 * k) & (lane < 8 * k + 8)
            r, l = roll(st[c, 1, at, :], 8 * k - 120), roll(st[c, 0, at, :], 8 * k)
            right = r if right is None else jnp.where(mine, r, right)
            left = l if left is None else jnp.where(mine, l, left)
        rpack[c] = right
        lpack[c] = left
        for k in range(8):
            near, far = st[c, 1, chunk(BASE + 8 * k), :], st[c, 1, chunk(BASE + 64 + 8 * k), :]
            rslab[c, chunk(8 * k), :] = jnp.where(lane < 64, roll(far, 64), near)
        for k in range(4):
            near, far = st[c, 1, chunk(BASE + 64 + 8 * k), :], st[c, 1, chunk(BASE + 96 + 8 * k), :]
            drslab[c, chunk(8 * k), :] = jnp.where(lane < 64, roll(far, 64), near)

    pl.semaphore_wait(barrier, 8)
    both = pl.ds(0, 2)
    messages = [
        ((0, 1), rpack, lr),
        ((0, -1), lpack, rl),
        ((1, 0), st.at[:, both, pl.ds(BASE + 112, 16), :], st.at[:, both, pl.ds(BASE - 16, 16), :]),
        ((-1, 0), st.at[:, both, pl.ds(BASE, 8), :], st.at[:, both, pl.ds(BASE + 128, 8), :]),
        ((1, 1), st.at[:, 1, pl.ds(BASE + 120, 8), :], ulc),
        ((1, -1), lpack, url),
        ((-1, 1), st.at[:, 1, pl.ds(BASE, 8), :], dlc),
        ((-1, -1), st.at[:, 0, pl.ds(BASE, 8), :], drc),
        ((0, 1), rslab, lslab),
        ((1, 1), drslab, ulslab),
        ((1, 0), st.at[:, both, pl.ds(BASE + 64, 48), :], st.at[:, both, pl.ds(0, 48), :]),
        ((0, 1), cnt_s, cnt.at[0]),
        ((0, -1), cnt_s, cnt.at[1]),
        ((1, 0), cnt_s, cnt.at[2]),
        ((-1, 0), cnt_s, cnt.at[3]),
        ((1, -1), cnt_s, cnt.at[4]),
        ((-1, 1), cnt_s, cnt.at[5]),
        ((-1, -1), cnt_s, cnt.at[6]),
    ]
    copies = [
        pltpu.make_async_remote_copy(
            src_ref=src, dst_ref=dst, send_sem=send_sem.at[i], recv_sem=recv_sem.at[i],
            device_id=device(*to), device_id_type=MESH,
        )
        for i, (to, src, dst) in enumerate(messages)
    ]
    for copy in copies:
        copy.start()
    for copy in copies[:8]:
        copy.wait_recv()

    for c in range(3):
        for k in range(-8, 17):
            if k < 0:
                right = roll(url[c], -8 * (k + 16))
            elif k < 16:
                right = roll(rl[c], -8 * k)
            else:
                right = drc[c]
            if k < -1:
                value = right
            else:
                left = ulc[c] if k < 0 else dlc[c] if k == 16 else roll(lr[c], 120 - 8 * k)
                value = jnp.where(lane < 64, right, left)
            st[c, 2, chunk(BASE + 8 * k), :] = value

    speed_pass(st, vel, 3, 7, 25)
    step_pass(st, vel, fine1, 3, 3, 7, 25)
    speed_pass(fine1, vel, 3, 7, 25)
    step_pass(fine1, vel, fine2, 3, 2, 8, 24)

    def coarsen(i, carry):
        for c in range(3):
            parts = coarse_rows(st, pl.multiple_of(BASE - 16 + 16 * i, 16), 3, c)
            for g in range(2):
                cgrid[c, g, chunk(pl.multiple_of(8 * i, 8)), :] = parts[g]
        return carry

    lax.fori_loop(0, 10, coarsen, 0)
    speed_pass(cgrid, cvel, 2, 0, 10)
    step_pass(cgrid, cvel, cone, 2, 1, 1, 9)

    def estimate(i, carry):
        total = None
        for c in range(3):
            fine = coarse_rows(fine2, pl.multiple_of(BASE + 16 * i, 16), 2, c)[0]
            gap = jnp.abs(fine - cone[c, 0, chunk(pl.multiple_of(8 * i + 8, 8)), :])
            total = gap if total is None else total + gap
        err[chunk(pl.multiple_of(8 * i, 8)), :] = 10.0 * total
        return carry

    lax.fori_loop(0, 8, estimate, 0)

    for copy in copies[8:]:
        copy.wait_recv()
    for copy in copies:
        copy.wait_send()


def patch_kernel(
    row_count, col_count, pos, ext, cnt, st, lslab, ulslab, dlc, err_in,
    err, moved, refined,
    lext, tiles, win, wvel, ctr, dcol, plus, base, mid, low,
):
    lane = lanes()
    row8 = lax.broadcasted_iota(jnp.int32, (8, 128), 0)
    err[...] = err_in[...]
    rc, cc = row_count[0, 0], col_count[0, 0]
    rc_of = lambda i: cnt[i, 0, 0]
    cc_of = lambda i: cnt[i, 0, 1]
    rows_in = (rc_of(0), rc, rc, rc_of(1))
    rows_below = (rc_of(5), rc_of(3), rc_of(3), rc_of(6))
    cols_in = {"up": (cc_of(2), cc_of(4)), "own": (cc, cc_of(1)), "down": (cc_of(3), cc_of(6))}

    for c in range(3):
        for k in range(8):
            x = lslab[c, chunk(8 * k), :]
            lext[c, chunk(BASE + 8 * k), :] = x
            lext[c, chunk(BASE + 64 + 8 * k), :] = roll(x, 64)
        for k in range(4):
            x = ulslab[c, chunk(8 * k), :]
            lext[c, chunk(8 * k), :] = x
            lext[c, chunk(32 + 8 * k), :] = roll(x, 64)
        lext[c, chunk(BASE + 128), :] = dlc[c]

    for c in range(3):
        columns = [lext.at[c], st.at[c, 0], st.at[c, 1], st.at[c, 2]]
        for k in range(-1, 17):
            at = chunk(BASE + 8 * k)
            values = [ref[at, :] for ref in columns]
            if 0 <= k < 8 or k == 16:
                counts = rows_below if k == 16 else rows_in
                first = 0 if k == 16 else 8 * k
                for g in range(4):
                    above = columns[g][chunk(BASE + 8 * k - counts[g]), :]
                    values[g] = jnp.where(row8 + first < counts[g], above, values[g])
            c0, c_right = cols_in["up" if k < 0 else "down" if k == 16 else "own"]
            m0 = jnp.where(lane < c0, roll(values[0], c0), values[1])
            m_right = jnp.where(lane < c_right, roll(values[2], c_right), values[3])
            put = chunk(8 * k + 8)
            for g, value in enumerate((values[0], m0, values[2], m_right)):
                tiles[g, c, put, :] = value
            if 0 <= k < 16:
                moved[c, chunk(8 * k), pl.ds(0, 128)] = m0
                moved[c, chunk(8 * k), pl.ds(128, 128)] = values[2]

    p0, p1 = pos[0, 0, 0], pos[0, 0, 1]
    group = lax.shift_right_logical(p1 + 126, 7)
    offset = lax.bitwise_and(p1 + 126, 127)
    back = lax.bitwise_and(128 - offset, 127)
    for k in range(10):
        u = []
        for c in range(3):
            at = chunk(p0 + 8 * k)
            a, b = tiles[group, c, at, :], tiles[group + 1, c, at, :]
            u.append(jnp.where(lane < 128 - offset, roll(a, back), roll(b, back)))
            win[c, chunk(8 * k + 8), :] = u[c]
        for c, value in enumerate(speeds(*u)):
            wvel[c, chunk(8 * k + 8), :] = value

    front = lane < 64
    for k in range(10):
        row = 8 * k + 8

        def load(shift, normal):
            at = chunk(row + shift)
            return side([win[c, at, :] for c in range(3)], [wvel[c, at, :] for c in range(3)], normal)

        here = load(0, 1)
        down, up = face(load(-1, 1), here), face(here, load(1, 1))
        across = load(0, 2)
        lower = (
            [roll(x, 1) for x in across[0]],
            [roll(x, 1) for x in across[1]],
            roll(across[2], 1),
        )
        left = face(lower, across)
        right = [roll(x, 127) for x in left]
        for a in range(2):
            far = []
            for c in range(3):
                twice = 2.0 * here[1][c]
                tall = up[c] - twice if a else twice - down[c]
                mid_c = here[0][c] - HALF * tall
                twice = 2.0 * across[1][c]
                e = mid_c - HALF * (twice - left[c])
                o = mid_c - HALF * (right[c] - twice)
                center = jnp.where(front, roll(e, -2), roll(o, 62))
                ctr[a, c, chunk(row), :] = center
                if 1 <= k < 9:
                    e62, o2 = roll(e, 62), roll(o, -1)
                    l1 = jnp.where(front, o2, e62)
                    r1 = jnp.where(front, roll(o, -2), roll(e, 61))
                    l2 = jnp.where(front, roll(e, -1), roll(o, 63))
                    r2 = jnp.where(front, roll(e, -3), roll(o, 61))
                    d1, d2, d3, d4 = l1 - l2, center - l1, r1 - center, r2 - r1
                    s_l, s_c, s_r = minmod(d1, d2), minmod(d2, d3), minmod(d3, d4)
                    far.append(
                        (l1 + 0.5 * s_l, center - 0.5 * s_c, center + 0.5 * s_c, r1 - 0.5 * s_r)
                    )
            if 1 <= k < 9:
                sides = [[far[c][i] for c in range(3)] for i in range(4)]
                sides = [side(s, speeds(*s), 2) for s in sides]
                f_low, f_high = face(sides[0], sides[1]), face(sides[2], sides[3])
                for c in range(3):
                    dcol[a, c, chunk(row), :] = f_high[c] - f_low[c]

    for k in range(10):
        row = 8 * k + 8
        at = chunk(row)
        l_side, r_side = [], []
        for c in range(3):
            c0, c1 = ctr[0, c, at, :], ctr[1, c, at, :]
            inner = c1 - c0
            before = c0 - ctr[1, c, chunk(row - 1), :]
            after = ctr[0, c, chunk(row + 1), :] - c1
            s0, s1 = minmod(before, inner), minmod(inner, after)
            base[c, at, :] = c0 - 0.5 * s0
            plus[c, at, :] = c1 + 0.5 * s1
            l_side.append(c0 + 0.5 * s0)
            r_side.append(c1 - 0.5 * s1)
        if 1 <= k < 9:
            f = face(side(l_side, speeds(*l_side), 1), side(r_side, speeds(*r_side), 1))
            for c in range(3):
                mid[c, at, :] = f[c]
    for k in range(1, 10):
        row = 8 * k + 8
        l_side = [plus[c, chunk(row - 1), :] for c in range(3)]
        r_side = [base[c, chunk(row), :] for c in range(3)]
        f = face(side(l_side, speeds(*l_side), 1), side(r_side, speeds(*r_side), 1))
        for c in range(3):
            low[c, chunk(row), :] = f[c]
    spread = lax.shift_right_logical(lane, 1) + 64 * lax.bitwise_and(lane, 1)
    inside_col = lax.bitwise_and(lane, 63) < ext[0, 0, 1]
    for k in range(1, 9):
        row = 8 * k + 8
        inside = inside_col & (row8 + 8 * (k - 1) < ext[0, 0, 0])
        for c in range(3):
            at = chunk(row)
            f_mid, f_low, f_next = mid[c, at, :], low[c, at, :], low[c, chunk(row + 1), :]
            for a, tall in enumerate((f_mid - f_low, f_next - f_mid)):
                done = ctr[a, c, at, :] - HALF * (tall + dcol[a, c, at, :])
                done = jnp.where(inside, done, 0.0)
                refined[c, pl.ds(16 * (k - 1) + a, 8, stride=2), :] = jnp.take_along_axis(
                    done, spread, axis=1, mode="promise_in_bounds"
                )


def solution(mesh):
    n_row, n_col = mesh.shape["row"], mesh.shape["col"]
    vmem = pl.BlockSpec(memory_space=pltpu.VMEM)
    smem = pl.BlockSpec(memory_space=pltpu.SMEM)
    buf = lambda *shape: pltpu.VMEM(shape, F32)

    def per_device(state, row_count, col_count, patch_pos, patch_ext):
        st, lslab, ulslab, dlc, cnt, err = pl.pallas_call(
            functools.partial(exchange_kernel, n_row, n_col),
            out_shape=(
                buf(3, 3, ROWS, 128),
                buf(3, 64, 128),
                buf(3, 32, 128),
                buf(3, 8, 128),
                jax.ShapeDtypeStruct((7, 1, 128), jnp.int32),
                buf(64, 128),
            ),
            in_specs=[pl.BlockSpec(memory_space=pl.ANY), smem, smem],
            out_specs=(vmem,) * 6,
            scratch_shapes=[
                buf(3, 8, 128), buf(3, 8, 128), buf(3, 64, 128), buf(3, 32, 128),
                pltpu.VMEM((1, 128), jnp.int32),
                *([buf(3, 8, 128)] * 5),
                buf(3, 3, ROWS, 128), buf(3, 3, ROWS, 128), buf(3, 2, ROWS, 128),
                buf(3, 2, 88, 128), buf(3, 2, 88, 128), buf(3, 1, 88, 128),
                pltpu.SemaphoreType.DMA((2,)),
                pltpu.SemaphoreType.DMA((N_MSG,)),
                pltpu.SemaphoreType.DMA((N_MSG,)),
            ],
            compiler_params=pltpu.CompilerParams(
                collective_id=0, has_side_effects=True, vmem_limit_bytes=24 << 20
            ),
        )(state, row_count, col_count)
        return pl.pallas_call(
            patch_kernel,
            out_shape=(
                jax.ShapeDtypeStruct((64, 128), F32),
                jax.ShapeDtypeStruct((3, 128, 256), F32),
                jax.ShapeDtypeStruct((3, 128, 128), F32),
            ),
            in_specs=[smem] * 5 + [vmem] * 5,
            out_specs=(vmem,) * 3,
            scratch_shapes=[
                buf(3, ROWS, 128), buf(4, 3, 144, 128), buf(3, 96, 128), buf(3, 96, 128),
                buf(2, 3, 96, 128), buf(2, 3, 96, 128),
                buf(3, 96, 128), buf(3, 96, 128), buf(3, 96, 128), buf(3, 96, 128),
            ],
            compiler_params=pltpu.CompilerParams(vmem_limit_bytes=24 << 20),
        )(row_count, col_count, patch_pos, patch_ext, cnt, st, lslab, ulslab, dlc, err)

    return jax.shard_map(
        per_device,
        mesh=mesh,
        in_specs=(
            P(None, "row", "col"),
            P("row", "col"),
            P("row", "col"),
            P("row", "col", None),
            P("row", "col", None),
        ),
        out_specs=(P("row", "col"), P(None, "row", "col"), P(None, "row", "col")),
        check_vma=False,
    )
```

time: 272 us -> 33.2 us (0.12)
  the two profiles are of different devices: /device:TPU:57 before, /device:TPU:1 now
where the time goes in v1:
time: 33.2 us; the launch traced here: 33 us
  Pallas kernels  29.4 us (89%)
  between operations  1.96 us (6%)
  local copies, waits for them, and re-layouts  1.65 us (5%)
    pallas_call x1, Pallas kernels, per_device(): pl.pallas_call(functools.partial(exchange_kernel, n_row, n_col), out_shap...  25.9 us
    pallas_call x1, Pallas kernels, per_device(): pl.pallas_call(patch_kernel, out_shape=(jax.ShapeDtypeStruct((64, 128), F...  3.5 us
    unnamed x6, local copies, waits for them, and re-layouts  1.65 us

profile of v1, /device:TPU:1, one launch (start us, length us, event | category | flops | bytes accessed | tf_op | source)
XLA Modules:
  0.0 33.0 jit_solution(7208315741897767285)
XLA Ops:
  1.9 0.0 copy-start
  1.9 1.0 %copy-done = f32[3,128,256]{2,1,0:T(8,128)S(1)} copy-done((f32[3,128,256]{2,1,0:T(8,128)S(1)}, f32[3,128,256]{2,1,0:T(8,128)}, u32[]{:S(2)}) %copy-start) | copy-done | bytes 393240
  2.9 25.9 %shard_map.76 = (f32[3,3,208,128]{3,2,1,0:T(8,128)S(1)}, f32[3,64,128]{2,1,0:T(8,128)S(1)}, f32[3,32,128]{2,1,0:T(8,128)S(1)}, f32[3,8,128]{2,1,0:T(8,128)S(1)},...) custom-call(f32[3,128,256]{2,1,0:T(8,128)S(1)} %copy-done, s32[1,1]{1,0:T(1,128)S(6)} %copy.8.row_count, ...), custom_call_target="tpu_custom_call" | custom-call | tf_op jit(solution)/shard_map/pallas_call | solution.py:415
  28.9 0.0 copy-start.1
  28.9 0.0 copy-start.2
  28.9 0.6 %copy-done.1 = s32[1,1,2]{2,1,0:T(1,128)S(1)} copy-done((s32[1,1,2]{2,1,0:T(1,128)S(1)}, s32[1,1,2]{2,1,0:T(1,128)}, u32[]{:S(2)}) %copy-start.1) | copy-done | bytes 32
  29.5 0.0 copy-done.2
  29.5 3.5 %shard_map.77 = (f32[64,128]{1,0:T(8,128)}, f32[3,128,256]{2,1,0:T(8,128)}, f32[3,128,128]{2,1,0:T(8,128)}) custom-call(s32[1,1]{1,0:T(1,128)S(6)} %copy.8.row_count, s32[1,1]{1,0:T(1,128)S(6)} %copy.9.col_count, s32[1,1,2]{2,1,0:T(1,128)S(1)} %copy-done.1, s32[1,1,2]{2,1,0:T(1,128)S(1)} %copy-done.2, s32[7,1,128]{2,1,0:T(1,128)S(1)} %get-tuple-element.9.cnt, ...), custom_call_target="tpu_custom_call" | custom-call | tf_op jit(solution)/shard_map/pallas_call | solution.py:441
Async XLA Ops:
  1.9 1.0 %copy-start = (f32[3,128,256]{2,1,0:T(8,128)S(1)}, f32[3,128,256]{2,1,0:T(8,128)}, u32[]{:S(2)}) copy-start(f32[3,128,256]{2,1,0:T(8,128)} %state.1) | copy-start | bytes 1179652
  28.9 0.7 %copy-start.1 = (s32[1,1,2]{2,1,0:T(1,128)S(1)}, s32[1,1,2]{2,1,0:T(1,128)}, u32[]{:S(2)}) copy-start(s32[1,1,2]{2,1,0:T(1,128)} %pos.1) | copy-start | bytes 28
  28.9 0.7 %copy-start.2 = (s32[1,1,2]{2,1,0:T(1,128)S(1)}, s32[1,1,2]{2,1,0:T(1,128)}, u32[]{:S(2)}) copy-start(s32[1,1,2]{2,1,0:T(1,128)} %ext.1) | copy-start | bytes 28

commit v2 on v1

--- a/solution.py
+++ b/solution.py
@@ -75,7 +75,7 @@
                 vel[k, g, at, :] = value
         return carry
 
-    lax.fori_loop(first, last, body, 0)
+    lax.fori_loop(first, last, body, 0, unroll=True)
 
 
 def step_pass(src, vel, dst, groups, keep, first, last):
@@ -113,7 +113,7 @@
                 dst[c, g, chunk(row), :] = here[0][c] - HALF * change
         return carry
 
-    lax.fori_loop(first, last, body, 0)
+    lax.fori_loop(first, last, body, 0, unroll=True)
 
 
 def coarse_rows(src, row, groups, c):
@@ -128,11 +128,11 @@
 
 
 def exchange_kernel(
-    n_row, n_col, state, row_count, col_count,
-    st, lslab, ulslab, dlc, cnt, err,
+    n_row, n_col, state, row_count, col_count, pos_hbm, ext_hbm,
+    st, lslab, ulslab, dlc, counts, pos, ext, err,
     rpack, lpack, rslab, drslab, cnt_s, lr, rl, url, ulc, drc,
     vel, fine1, fine2, cgrid, cvel, cone,
-    local_sem, send_sem, recv_sem,
+    cnt, local_sem, send_sem, recv_sem,
 ):
     me_r, me_c = lax.axis_index("row"), lax.axis_index("col")
 
@@ -145,8 +145,12 @@
         )
         for g in range(2)
     ]
-    loads[1].start()
-    loads[0].start()
+    loads += [
+        pltpu.make_async_copy(pos_hbm, pos, local_sem.at[2]),
+        pltpu.make_async_copy(ext_hbm, ext, local_sem.at[3]),
+    ]
+    for load in loads:
+        load.start()
     barrier = pltpu.get_barrier_semaphore()
     around = [(a, b) for a in (-1, 0, 1) for b in (-1, 0, 1) if (a, b) != (0, 0)]
     for a, b in around:
@@ -154,9 +158,9 @@
 
     lane = lanes()
     lane1 = lanes((1, 128))
-    cnt_s[...] = jnp.where(lane1 == 0, row_count[0, 0], col_count[0, 0])
-    loads[1].wait()
-    loads[0].wait()
+    cnt_s[...] = jnp.where(lane1 == 0, row_count[...], col_count[...])
+    for load in loads:
+        load.wait()
     for c in range(3):
         right = left = None
         for k in range(16):
@@ -235,7 +239,7 @@
                 cgrid[c, g, chunk(pl.multiple_of(8 * i, 8)), :] = parts[g]
         return carry
 
-    lax.fori_loop(0, 10, coarsen, 0)
+    lax.fori_loop(0, 10, coarsen, 0, unroll=True)
     speed_pass(cgrid, cvel, 2, 0, 10)
     step_pass(cgrid, cvel, cone, 2, 1, 1, 9)
 
@@ -248,29 +252,30 @@
         err[chunk(pl.multiple_of(8 * i, 8)), :] = 10.0 * total
         return carry
 
-    lax.fori_loop(0, 8, estimate, 0)
+    lax.fori_loop(0, 8, estimate, 0, unroll=True)
 
     for copy in copies[8:]:
         copy.wait_recv()
+    keep = [
+        pltpu.make_async_copy(cnt, counts.at[pl.ds(0, 7)], local_sem.at[0]),
+        pltpu.make_async_copy(cnt_s, counts.at[7], local_sem.at[1]),
+    ]
+    for copy in keep:
+        copy.start()
     for copy in copies:
         copy.wait_send()
+    for copy in keep:
+        copy.wait()
 
 
 def patch_kernel(
-    row_count, col_count, pos, ext, cnt, st, lslab, ulslab, dlc, err_in,
+    cnt, pos, ext, st, lslab, ulslab, dlc, err_in,
     err, moved, refined,
     lext, tiles, win, wvel, ctr, dcol, plus, base, mid, low,
 ):
     lane = lanes()
     row8 = lax.broadcasted_iota(jnp.int32, (8, 128), 0)
     err[...] = err_in[...]
-    rc, cc = row_count[0, 0], col_count[0, 0]
-    rc_of = lambda i: cnt[i, 0, 0]
-    cc_of = lambda i: cnt[i, 0, 1]
-    rows_in = (rc_of(0), rc, rc, rc_of(1))
-    rows_below = (rc_of(5), rc_of(3), rc_of(3), rc_of(6))
-    cols_in = {"up": (cc_of(2), cc_of(4)), "own": (cc, cc_of(1)), "down": (cc_of(3), cc_of(6))}
-
     for c in range(3):
         for k in range(8):
             x = lslab[c, chunk(8 * k), :]
@@ -281,6 +286,13 @@
             lext[c, chunk(8 * k), :] = x
             lext[c, chunk(32 + 8 * k), :] = roll(x, 64)
         lext[c, chunk(BASE + 128), :] = dlc[c]
+
+    rc, cc = cnt[7, 0, 0], cnt[7, 0, 1]
+    rc_of = lambda i: cnt[i, 0, 0]
+    cc_of = lambda i: cnt[i, 0, 1]
+    rows_in = (rc_of(0), rc, rc, rc_of(1))
+    rows_below = (rc_of(5), rc_of(3), rc_of(3), rc_of(6))
+    cols_in = {"up": (cc_of(2), cc_of(4)), "own": (cc, cc_of(1)), "down": (cc_of(3), cc_of(6))}
 
     for c in range(3):
         columns = [lext.at[c], st.at[c, 0], st.at[c, 1], st.at[c, 2]]
@@ -409,35 +421,43 @@
     n_row, n_col = mesh.shape["row"], mesh.shape["col"]
     vmem = pl.BlockSpec(memory_space=pltpu.VMEM)
     smem = pl.BlockSpec(memory_space=pltpu.SMEM)
+    hbm = pl.BlockSpec(memory_space=pltpu.HBM)
     buf = lambda *shape: pltpu.VMEM(shape, F32)
 
     def per_device(state, row_count, col_count, patch_pos, patch_ext):
-        st, lslab, ulslab, dlc, cnt, err = pl.pallas_call(
+        in_hbm = [
+            x if x.ndim == 2 else pltpu.with_memory_space_constraint(x, pltpu.HBM)
+            for x in (state, row_count, col_count, patch_pos, patch_ext)
+        ]
+        st, lslab, ulslab, dlc, cnt, pos, ext, err = pl.pallas_call(
             functools.partial(exchange_kernel, n_row, n_col),
             out_shape=(
                 buf(3, 3, ROWS, 128),
                 buf(3, 64, 128),
                 buf(3, 32, 128),
                 buf(3, 8, 128),
-                jax.ShapeDtypeStruct((7, 1, 128), jnp.int32),
+                pltpu.SMEM((8, 1, 128), jnp.int32),
+                pltpu.SMEM((1, 1, 2), jnp.int32),
+                pltpu.SMEM((1, 1, 2), jnp.int32),
                 buf(64, 128),
             ),
-            in_specs=[pl.BlockSpec(memory_space=pl.ANY), smem, smem],
-            out_specs=(vmem,) * 6,
+            in_specs=[hbm, vmem, vmem, hbm, hbm],
+            out_specs=(vmem,) * 4 + (smem,) * 3 + (vmem,),
             scratch_shapes=[
                 buf(3, 8, 128), buf(3, 8, 128), buf(3, 64, 128), buf(3, 32, 128),
                 pltpu.VMEM((1, 128), jnp.int32),
                 *([buf(3, 8, 128)] * 5),
                 buf(3, 3, ROWS, 128), buf(3, 3, ROWS, 128), buf(3, 2, ROWS, 128),
                 buf(3, 2, 88, 128), buf(3, 2, 88, 128), buf(3, 1, 88, 128),
-                pltpu.SemaphoreType.DMA((2,)),
+                pltpu.VMEM((7, 1, 128), jnp.int32),
+                pltpu.SemaphoreType.DMA((4,)),
                 pltpu.SemaphoreType.DMA((N_MSG,)),
                 pltpu.SemaphoreType.DMA((N_MSG,)),
             ],
             compiler_params=pltpu.CompilerParams(
                 collective_id=0, has_side_effects=True, vmem_limit_bytes=24 << 20
             ),
-        )(state, row_count, col_count)
+        )(*in_hbm)
         return pl.pallas_call(
             patch_kernel,
             out_shape=(
@@ -445,7 +465,7 @@
                 jax.ShapeDtypeStruct((3, 128, 256), F32),
                 jax.ShapeDtypeStruct((3, 128, 128), F32),
             ),
-            in_specs=[smem] * 5 + [vmem] * 5,
+            in_specs=[smem] * 3 + [vmem] * 5,
             out_specs=(vmem,) * 3,
             scratch_shapes=[
                 buf(3, ROWS, 128), buf(4, 3, 144, 128), buf(3, 96, 128), buf(3, 96, 128),
@@ -453,7 +473,7 @@
                 buf(3, 96, 128), buf(3, 96, 128), buf(3, 96, 128), buf(3, 96, 128),
             ],
             compiler_params=pltpu.CompilerParams(vmem_limit_bytes=24 << 20),
-        )(row_count, col_count, patch_pos, patch_ext, cnt, st, lslab, ulslab, dlc, err)
+        )(cnt, pos, ext, st, lslab, ulslab, dlc, err)
 
     return jax.shard_map(
         per_device,

time: 33.2 us -> 26.7 us (0.80)
  Pallas kernels: 29.4 us -> 24.5 us
  local copies, waits for them, and re-layouts: 1.65 us -> 0 us
    pallas_call x1, Pallas kernels: 25.9 us -> 21.6 us  [per_device(): pl.pallas_call(functools.partial(exchange_kernel, n_row, n_col), out_shap...]
    unnamed x6 -> x0, local copies, waits for them, and re-layouts: 1.65 us -> none
    pallas_call x1, Pallas kernels: 3.5 us -> 2.9 us  [per_device(): pl.pallas_call(patch_kernel, out_shape=(jax.ShapeDtypeStruct((64, 128), F...]
where the time goes in v2:
time: 26.7 us; the launch traced here: 26.4 us
  Pallas kernels  24.5 us (92%)
  between operations  1.93 us (7%)
    pallas_call x1, Pallas kernels, per_device(): pl.pallas_call(functools.partial(exchange_kernel, n_row, n_col), out_shap...  21.6 us
    pallas_call x1, Pallas kernels, per_device(): pl.pallas_call(patch_kernel, out_shape=(jax.ShapeDtypeStruct((64, 128), F...  2.9 us

profile of v2, /device:TPU:1, one launch (start us, length us, event | category | flops | bytes accessed | tf_op | source)
XLA Modules:
  0.0 26.4 jit_solution(8996596829478347620)
XLA Ops:
  1.9 21.6 %shard_map.76 = (f32[3,3,208,128]{3,2,1,0:T(8,128)S(1)}, f32[3,64,128]{2,1,0:T(8,128)S(1)}, f32[3,32,128]{2,1,0:T(8,128)S(1)}, f32[3,8,128]{2,1,0:T(8,128)S(1)},...) custom-call(f32[3,128,256]{2,1,0:T(8,128)} %state.1, ...), custom_call_target="tpu_custom_call" | custom-call | tf_op jit(solution)/shard_map/pallas_call | solution.py:432
  23.5 2.9 %shard_map.77 = (f32[64,128]{1,0:T(8,128)}, f32[3,128,256]{2,1,0:T(8,128)}, f32[3,128,128]{2,1,0:T(8,128)}) custom-call(s32[8,1,128]{2,1,0:T(1,128)S(4)} %get-tuple-element.11.cnt, s32[1,1,2]{2,1,0:T(1,128)S(4)} %get-tuple-element.12.pos, s32[1,1,2]{2,1,0:T(1,128)S(4)} %get-tuple-element.13.ext, f32[3,3,208,128]{3,2,1,0:T(8,128)S(1)} %get-tuple-element.14.st, ...), custom_call_target="tpu_custom_call" | custom-call | tf_op jit(solution)/shard_map/pallas_call | solution.py:461

commit v3 on v2

--- a/solution.py
+++ b/solution.py
@@ -9,7 +9,6 @@
 
 MESH = pl.DeviceIdType.MESH
 F32 = jnp.float32
-SLAB = 64
 HALF = 0.05
 BASE = 64
 ROWS = 208
@@ -68,21 +67,17 @@
 
 
 def speed_pass(src, vel, groups, first, last):
-    def body(i, carry):
-        at = chunk(pl.multiple_of(i * 8, 8))
-        for g in range(groups):
+    for i in range(first, last):
+        at = chunk(8 * i)
+        for g in groups:
             for k, value in enumerate(speeds(*(src[c, g, at, :] for c in range(3)))):
                 vel[k, g, at, :] = value
-        return carry
-
-    lax.fori_loop(first, last, body, 0, unroll=True)
-
-
-def step_pass(src, vel, dst, groups, keep, first, last):
+
+
+def step_pass(src, vel, dst, groups, first, last):
     lane = lanes()
-
-    def body(i, carry):
-        row = pl.multiple_of(i * 8, 8)
+    for i in range(first, last):
+        row = 8 * i
 
         def load(shift, g, normal):
             at = chunk(row + shift)
@@ -92,46 +87,33 @@
                 normal,
             )
 
-        along = [load(0, g, 2) for g in range(groups)]
-        flat = [[*s[0], s[1][0], s[1][1], s[1][2], s[2]] for s in along]
-        shifted = [
-            from_lower([flat[g][k] for g in range(groups)], lane)
-            for k in (0, 1, 2, 4, 5, 6)
-        ]
+        along = [load(0, g, 2) for g in groups]
+        shifted = [from_lower([a[0][k] for a in along], lane) for k in range(3)]
         low = []
-        for g in range(groups):
-            u = [shifted[k][g] for k in range(3)]
-            lower = (u, (u[2], shifted[3][g], shifted[4][g]), shifted[5][g])
-            low.append(face(lower, along[g]))
-        high = [from_upper([low[g][c] for g in range(groups)], lane) for c in range(3)]
-        for g in range(keep):
+        for n in range(len(groups)):
+            u = [x[n] for x in shifted]
+            low.append(face(side(u, speeds(*u), 2), along[n]))
+        high = [from_upper([f[c] for f in low], lane) for c in range(3)]
+        for n, g in enumerate(groups):
             here = load(0, g, 1)
             down = face(load(-1, g, 1), here)
             up = face(here, load(1, g, 1))
             for c in range(3):
-                change = (up[c] - down[c]) + (high[c][g] - low[g][c])
+                change = (up[c] - down[c]) + (high[c][n] - low[n][c])
                 dst[c, g, chunk(row), :] = here[0][c] - HALF * change
-        return carry
-
-    lax.fori_loop(first, last, body, 0, unroll=True)
-
-
-def coarse_rows(src, row, groups, c):
-    lane = lanes()
-    even = lax.rem(2 * lane, 128)
-    out = []
-    for g in range(groups):
-        pair = src[c, g, pl.ds(row, 8, stride=2), :] + src[c, g, pl.ds(row + 1, 8, stride=2), :]
-        pair = pair + roll(pair, 127)
-        out.append(jnp.take_along_axis(pair, even, axis=1, mode="promise_in_bounds"))
-    return [0.25 * jnp.where(lane < 64, out[0], out[1])] + [0.25 * x for x in out[2:]]
+
+
+def coarse_rows(src, row, g, c, even):
+    pair = src[c, g, pl.ds(row, 8, stride=2), :] + src[c, g, pl.ds(row + 1, 8, stride=2), :]
+    pair = pair + roll(pair, 127)
+    return 0.25 * jnp.take_along_axis(pair, even, axis=1, mode="promise_in_bounds")
 
 
 def exchange_kernel(
     n_row, n_col, state, row_count, col_count, pos_hbm, ext_hbm,
-    st, lslab, ulslab, dlc, counts, pos, ext, err,
-    rpack, lpack, rslab, drslab, cnt_s, lr, rl, url, ulc, drc,
-    vel, fine1, fine2, cgrid, cvel, cone,
+    st, rm, l_low, l_high, ulc, dlc, drc, counts, pos, ext, err,
+    rpack, lpack, low_s, high_s, cnt_s, lr, rl, url, up_low, ahead,
+    vel, rim, fine1, fine2, cgrid, cvel, cone,
     cnt, local_sem, send_sem, recv_sem,
 ):
     me_r, me_c = lax.axis_index("row"), lax.axis_index("col")
@@ -157,48 +139,54 @@
         pl.semaphore_signal(barrier, inc=1, device_id=device(a, b), device_id_type=MESH)
 
     lane = lanes()
-    lane1 = lanes((1, 128))
-    cnt_s[...] = jnp.where(lane1 == 0, row_count[...], col_count[...])
+    row8 = lax.broadcasted_iota(jnp.int32, (8, 128), 0)
+    rc = row_count[0, 0]
+    cnt_s[...] = jnp.where(lanes((1, 128)) == 0, rc, col_count[0, 0])
     for load in loads:
         load.wait()
-    for c in range(3):
-        right = left = None
-        for k in range(16):
-            at = chunk(BASE + 8 * k)
-            mine = (lane >= 8 * k) & (lane < 8 * k + 8)
-            r, l = roll(st[c, 1, at, :], 8 * k - 120), roll(st[c, 0, at, :], 8 * k)
-            right = r if right is None else jnp.where(mine, r, right)
-            left = l if left is None else jnp.where(mine, l, left)
-        rpack[c] = right
-        lpack[c] = left
-        for k in range(8):
-            near, far = st[c, 1, chunk(BASE + 8 * k), :], st[c, 1, chunk(BASE + 64 + 8 * k), :]
-            rslab[c, chunk(8 * k), :] = jnp.where(lane < 64, roll(far, 64), near)
+
+    def edge(columns, lane_at):
+        tile = None
+        for c in range(3):
+            for k in range(16):
+                to = 32 * c + 2 * k
+                x = roll(columns(c, k), to - lane_at)
+                tile = x if tile is None else jnp.where(lane >= to, x, tile)
+        return tile
+
+    def fold(low, high):
+        return jnp.where(lane < 64, roll(high, 64), low)
+
+    rpack[...] = edge(lambda c, k: st[c, 1, chunk(BASE + 8 * k), :], 126)
+    lpack[...] = edge(lambda c, k: st[c, 0, chunk(BASE + 8 * k), :], 0)
+    for c in range(3):
         for k in range(4):
-            near, far = st[c, 1, chunk(BASE + 64 + 8 * k), :], st[c, 1, chunk(BASE + 96 + 8 * k), :]
-            drslab[c, chunk(8 * k), :] = jnp.where(lane < 64, roll(far, 64), near)
+            low_s[c, chunk(8 * k), :] = fold(
+                st[c, 1, chunk(BASE + 64 + 8 * k), :], st[c, 1, chunk(BASE + 96 + 8 * k), :]
+            )
 
     pl.semaphore_wait(barrier, 8)
     both = pl.ds(0, 2)
+    head, tail = pl.ds(0, 2), pl.ds(6, 2)
     messages = [
+        ((1, 0), low_s, up_low),
         ((0, 1), rpack, lr),
         ((0, -1), lpack, rl),
         ((1, 0), st.at[:, both, pl.ds(BASE + 112, 16), :], st.at[:, both, pl.ds(BASE - 16, 16), :]),
         ((-1, 0), st.at[:, both, pl.ds(BASE, 8), :], st.at[:, both, pl.ds(BASE + 128, 8), :]),
-        ((1, 1), st.at[:, 1, pl.ds(BASE + 120, 8), :], ulc),
+        ((1, 1), st.at[:, 1, pl.ds(BASE + 126, 2), :], ulc.at[:, tail, :]),
         ((1, -1), lpack, url),
-        ((-1, 1), st.at[:, 1, pl.ds(BASE, 8), :], dlc),
-        ((-1, -1), st.at[:, 0, pl.ds(BASE, 8), :], drc),
-        ((0, 1), rslab, lslab),
-        ((1, 1), drslab, ulslab),
+        ((-1, 1), st.at[:, 1, pl.ds(BASE, 2), :], dlc.at[:, head, :]),
+        ((-1, -1), st.at[:, 0, pl.ds(BASE, 2), :], drc.at[:, head, :]),
+        ((0, 1), low_s, l_low),
         ((1, 0), st.at[:, both, pl.ds(BASE + 64, 48), :], st.at[:, both, pl.ds(0, 48), :]),
-        ((0, 1), cnt_s, cnt.at[0]),
-        ((0, -1), cnt_s, cnt.at[1]),
-        ((1, 0), cnt_s, cnt.at[2]),
-        ((-1, 0), cnt_s, cnt.at[3]),
-        ((1, -1), cnt_s, cnt.at[4]),
-        ((-1, 1), cnt_s, cnt.at[5]),
-        ((-1, -1), cnt_s, cnt.at[6]),
+        ((0, -1), cnt_s, cnt.at[0]),
+        ((1, 0), cnt_s, cnt.at[1]),
+        ((-1, 0), cnt_s, cnt.at[2]),
+        ((1, -1), cnt_s, cnt.at[3]),
+        ((-1, 1), cnt_s, cnt.at[4]),
+        ((-1, -1), cnt_s, cnt.at[5]),
+        ((0, 1), high_s, l_high),
     ]
     copies = [
         pltpu.make_async_remote_copy(
@@ -207,58 +195,119 @@
         )
         for i, (to, src, dst) in enumerate(messages)
     ]
-    for copy in copies:
+    for copy in copies[:17]:
         copy.start()
-    for copy in copies[:8]:
+
+    even = lax.rem(2 * lane, 128)
+    own = (0, 1)
+    speed_pass(st, vel, own, 8, 24)
+    step_pass(st, vel, fine1, own, 9, 23)
+
+    copies[0].wait_recv()
+    for c in range(3):
+        for k in range(4):
+            x = up_low[c, chunk(8 * k), :]
+            ahead[c, chunk(8 * k), :] = x
+            ahead[c, chunk(32 + 8 * k), :] = roll(x, 64)
+        for k in range(8):
+            ahead[c, chunk(64 + 8 * k), :] = st[c, 1, chunk(BASE + 8 * k), :]
+    for c in range(3):
+        top = [
+            jnp.where(
+                row8 + 8 * k < rc,
+                ahead[c, chunk(64 + 8 * k - rc), :],
+                ahead[c, chunk(64 + 8 * k), :],
+            )
+            for k in range(8)
+        ]
+        for k in range(4):
+            high_s[c, chunk(8 * k), :] = fold(top[k], top[k + 4])
+    copies[17].start()
+
+    def coarse_own(i):
+        for c in range(3):
+            halves = [coarse_rows(st, BASE - 16 + 16 * i, g, c, even) for g in range(2)]
+            cgrid[c, 0, chunk(8 * i), :] = jnp.where(lane < 64, *halves)
+        speed_pass(cgrid, cvel, (0,), i, i + 1)
+
+    def estimate(i):
+        total = None
+        for c in range(3):
+            halves = [coarse_rows(fine2, BASE + 16 * i, g, c, even) for g in range(2)]
+            gap = jnp.abs(jnp.where(lane < 64, *halves) - cone[c, 0, chunk(8 * i + 8), :])
+            total = gap if total is None else total + gap
+        err[chunk(8 * i), :] = 10.0 * total
+
+    speed_pass(fine1, vel, own, 9, 23)
+    step_pass(fine1, vel, fine2, own, 10, 22)
+    for i in range(1, 9):
+        coarse_own(i)
+    step_pass(cgrid, cvel, cone, (0,), 2, 8)
+    for i in range(1, 7):
+        estimate(i)
+
+    for copy in copies[1:9]:
         copy.wait_recv()
-
+    speed_pass(st, rim, own, 7, 10)
+    speed_pass(st, rim, own, 22, 25)
+    step_pass(st, rim, fine1, own, 7, 9)
+    step_pass(st, rim, fine1, own, 23, 25)
+    speed_pass(fine1, rim, own, 7, 11)
+    speed_pass(fine1, rim, own, 21, 25)
+    step_pass(fine1, rim, fine2, own, 8, 10)
+    step_pass(fine1, rim, fine2, own, 22, 24)
+    coarse_own(0)
+    coarse_own(9)
+    step_pass(cgrid, cvel, cone, (0,), 1, 2)
+    step_pass(cgrid, cvel, cone, (0,), 8, 9)
+    estimate(0)
+    estimate(7)
+
+    left, right, corner = lr[...], rl[...], url[...]
     for c in range(3):
         for k in range(-8, 17):
-            if k < 0:
-                right = roll(url[c], -8 * (k + 16))
-            elif k < 16:
-                right = roll(rl[c], -8 * k)
-            else:
-                right = drc[c]
-            if k < -1:
-                value = right
-            else:
-                left = ulc[c] if k < 0 else dlc[c] if k == 16 else roll(lr[c], 120 - 8 * k)
-                value = jnp.where(lane < 64, right, left)
-            st[c, 2, chunk(BASE + 8 * k), :] = value
-
-    speed_pass(st, vel, 3, 7, 25)
-    step_pass(st, vel, fine1, 3, 3, 7, 25)
-    speed_pass(fine1, vel, 3, 7, 25)
-    step_pass(fine1, vel, fine2, 3, 2, 8, 24)
-
-    def coarsen(i, carry):
-        for c in range(3):
-            parts = coarse_rows(st, pl.multiple_of(BASE - 16 + 16 * i, 16), 3, c)
-            for g in range(2):
-                cgrid[c, g, chunk(pl.multiple_of(8 * i, 8)), :] = parts[g]
-        return carry
-
-    lax.fori_loop(0, 10, coarsen, 0, unroll=True)
-    speed_pass(cgrid, cvel, 2, 0, 10)
-    step_pass(cgrid, cvel, cone, 2, 1, 1, 9)
-
-    def estimate(i, carry):
+            at = chunk(BASE + 8 * k)
+            col = 32 * c + 2 * k
+            r = roll(corner, -(col + 32)) if k < 0 else drc[c] if k == 16 else roll(right, -col)
+            if k >= -1:
+                ends = ulc[c] if k < 0 else dlc[c]
+                x = roll(left, 62 - col) if 0 <= k < 16 else roll(ends, 64)
+                x = jnp.where(lane < 64, x, roll(st[c, 0, at, :], 64))
+                r = jnp.where(lane < 32, r, jnp.where(lane < 124, x, st[c, 1, at, :]))
+            st[c, 2, at, :] = r
+    strip = (2,)
+    speed_pass(st, vel, strip, 7, 25)
+    step_pass(st, vel, fine1, strip, 7, 25)
+    speed_pass(fine1, vel, strip, 7, 25)
+    step_pass(fine1, vel, fine2, strip, 8, 24)
+    for i in range(10):
+        for c in range(3):
+            cgrid[c, 1, chunk(8 * i), :] = coarse_rows(st, BASE - 16 + 16 * i, 2, c, even)
+    speed_pass(cgrid, cvel, (1,), 0, 10)
+    step_pass(cgrid, cvel, cone, (1,), 1, 9)
+    for i in range(8):
         total = None
         for c in range(3):
-            fine = coarse_rows(fine2, pl.multiple_of(BASE + 16 * i, 16), 2, c)[0]
-            gap = jnp.abs(fine - cone[c, 0, chunk(pl.multiple_of(8 * i + 8, 8)), :])
+            fine = coarse_rows(fine2, BASE + 16 * i, 2, c, even)
+            gap = jnp.abs(fine - cone[c, 1, chunk(8 * i + 8), :])
             total = gap if total is None else total + gap
-        err[chunk(pl.multiple_of(8 * i, 8)), :] = 10.0 * total
-        return carry
-
-    lax.fori_loop(0, 8, estimate, 0, unroll=True)
-
-    for copy in copies[8:]:
+        total = 10.0 * total
+        at = chunk(8 * i)
+        value = jnp.where(lane == 127, total, err[at, :])
+        err[at, :] = jnp.where(lane == 0, roll(total, 96), value)
+
+    for copy in copies[9:17]:
         copy.wait_recv()
+    for c in range(3):
+        for g in range(2):
+            for k in range(8):
+                here = st[c, g, chunk(BASE + 8 * k), :]
+                above = st[c, g, chunk(BASE + 8 * k - rc), :]
+                rm[c, g, chunk(8 * k), :] = jnp.where(row8 + 8 * k < rc, above, here)
+    copies[17].wait_recv()
     keep = [
-        pltpu.make_async_copy(cnt, counts.at[pl.ds(0, 7)], local_sem.at[0]),
-        pltpu.make_async_copy(cnt_s, counts.at[7], local_sem.at[1]),
+        pltpu.make_async_copy(cnt, counts.at[pl.ds(0, 6)], local_sem.at[0]),
+        pltpu.make_async_copy(cnt_s, counts.at[6], local_sem.at[1]),
     ]
     for copy in keep:
         copy.start()
@@ -269,48 +318,55 @@
 
 
 def patch_kernel(
-    cnt, pos, ext, st, lslab, ulslab, dlc, err_in,
+    cnt, pos, ext, st, rm, l_low, l_high, ulc, dlc, err_in,
     err, moved, refined,
-    lext, tiles, win, wvel, ctr, dcol, plus, base, mid, low,
+    tiles, win, wvel, ctr, dcol, plus, base, mid, low,
 ):
     lane = lanes()
     row8 = lax.broadcasted_iota(jnp.int32, (8, 128), 0)
     err[...] = err_in[...]
-    for c in range(3):
-        for k in range(8):
-            x = lslab[c, chunk(8 * k), :]
-            lext[c, chunk(BASE + 8 * k), :] = x
-            lext[c, chunk(BASE + 64 + 8 * k), :] = roll(x, 64)
-        for k in range(4):
-            x = ulslab[c, chunk(8 * k), :]
-            lext[c, chunk(8 * k), :] = x
-            lext[c, chunk(32 + 8 * k), :] = roll(x, 64)
-        lext[c, chunk(BASE + 128), :] = dlc[c]
-
-    rc, cc = cnt[7, 0, 0], cnt[7, 0, 1]
     rc_of = lambda i: cnt[i, 0, 0]
     cc_of = lambda i: cnt[i, 0, 1]
-    rows_in = (rc_of(0), rc, rc, rc_of(1))
-    rows_below = (rc_of(5), rc_of(3), rc_of(3), rc_of(6))
-    cols_in = {"up": (cc_of(2), cc_of(4)), "own": (cc, cc_of(1)), "down": (cc_of(3), cc_of(6))}
-
-    for c in range(3):
-        columns = [lext.at[c], st.at[c, 0], st.at[c, 1], st.at[c, 2]]
+    rows_below = (rc_of(4), rc_of(2), rc_of(2), rc_of(5))
+    cols_in = {"up": (cc_of(1), cc_of(3)), "own": (cc_of(6), cc_of(0)), "down": (cc_of(2), cc_of(5))}
+
+    rc_right = rc_of(0)
+    for c in range(3):
+        for k in range(4):
+            for start, half in ((0, l_high), (64, l_low)):
+                x = half[c, chunk(8 * k), :]
+                tiles[0, c, chunk(8 + start + 8 * k), :] = x
+                tiles[0, c, chunk(40 + start + 8 * k), :] = roll(x, 64)
+        tiles[0, c, chunk(0), :] = ulc[c]
+
+    for c in range(3):
         for k in range(-1, 17):
             at = chunk(BASE + 8 * k)
-            values = [ref[at, :] for ref in columns]
-            if 0 <= k < 8 or k == 16:
-                counts = rows_below if k == 16 else rows_in
-                first = 0 if k == 16 else 8 * k
-                for g in range(4):
-                    above = columns[g][chunk(BASE + 8 * k - counts[g]), :]
-                    values[g] = jnp.where(row8 + first < counts[g], above, values[g])
+            if k < 0:
+                values = [ulc[c], st[c, 0, at, :], st[c, 1, at, :], st[c, 2, at, :]]
+            elif k < 16:
+                own = [rm[c, g, chunk(8 * k), :] if k < 8 else st[c, g, at, :] for g in range(2)]
+                beside = st[c, 2, at, :]
+                if k < 8:
+                    above = st[c, 2, chunk(BASE + 8 * k - rc_right), :]
+                    beside = jnp.where(row8 + 8 * k < rc_right, above, beside)
+                values = [tiles[0, c, chunk(8 * k + 8), :], *own, beside]
+            else:
+                above = [
+                    tiles[0, c, chunk(136 - rows_below[0]), :],
+                    st[c, 0, chunk(BASE + 128 - rows_below[1]), :],
+                    st[c, 1, chunk(BASE + 128 - rows_below[2]), :],
+                    st[c, 2, chunk(BASE + 128 - rows_below[3]), :],
+                ]
+                below = [dlc[c], st[c, 0, at, :], st[c, 1, at, :], st[c, 2, at, :]]
+                values = [jnp.where(row8 < rows_below[g], above[g], below[g]) for g in range(4)]
+                tiles[0, c, chunk(136), :] = values[0]
             c0, c_right = cols_in["up" if k < 0 else "down" if k == 16 else "own"]
             m0 = jnp.where(lane < c0, roll(values[0], c0), values[1])
             m_right = jnp.where(lane < c_right, roll(values[2], c_right), values[3])
             put = chunk(8 * k + 8)
-            for g, value in enumerate((values[0], m0, values[2], m_right)):
-                tiles[g, c, put, :] = value
+            for g, value in enumerate((m0, values[2], m_right)):
+                tiles[g + 1, c, put, :] = value
             if 0 <= k < 16:
                 moved[c, chunk(8 * k), pl.ds(0, 128)] = m0
                 moved[c, chunk(8 * k), pl.ds(128, 128)] = values[2]
@@ -429,27 +485,24 @@
             x if x.ndim == 2 else pltpu.with_memory_space_constraint(x, pltpu.HBM)
             for x in (state, row_count, col_count, patch_pos, patch_ext)
         ]
-        st, lslab, ulslab, dlc, cnt, pos, ext, err = pl.pallas_call(
+        corner = buf(3, 8, 128)
+        half = buf(3, 32, 128)
+        *parts, _, cnt, pos, ext, err = pl.pallas_call(
             functools.partial(exchange_kernel, n_row, n_col),
             out_shape=(
-                buf(3, 3, ROWS, 128),
-                buf(3, 64, 128),
-                buf(3, 32, 128),
-                buf(3, 8, 128),
-                pltpu.SMEM((8, 1, 128), jnp.int32),
+                buf(3, 3, ROWS, 128), buf(3, 2, 64, 128), half, half, *([corner] * 3),
+                pltpu.SMEM((7, 1, 128), jnp.int32),
                 pltpu.SMEM((1, 1, 2), jnp.int32),
                 pltpu.SMEM((1, 1, 2), jnp.int32),
                 buf(64, 128),
             ),
-            in_specs=[hbm, vmem, vmem, hbm, hbm],
-            out_specs=(vmem,) * 4 + (smem,) * 3 + (vmem,),
+            in_specs=[hbm, smem, smem, hbm, hbm],
+            out_specs=(vmem,) * 7 + (smem,) * 3 + (vmem,),
             scratch_shapes=[
-                buf(3, 8, 128), buf(3, 8, 128), buf(3, 64, 128), buf(3, 32, 128),
-                pltpu.VMEM((1, 128), jnp.int32),
-                *([buf(3, 8, 128)] * 5),
-                buf(3, 3, ROWS, 128), buf(3, 3, ROWS, 128), buf(3, 2, ROWS, 128),
-                buf(3, 2, 88, 128), buf(3, 2, 88, 128), buf(3, 1, 88, 128),
-                pltpu.VMEM((7, 1, 128), jnp.int32),
+                buf(8, 128), buf(8, 128), half, half, pltpu.VMEM((1, 128), jnp.int32),
+                buf(8, 128), buf(8, 128), buf(8, 128), half, buf(3, 128, 128),
+                *([buf(3, 3, ROWS, 128)] * 4), *([buf(3, 2, 88, 128)] * 3),
+                pltpu.VMEM((6, 1, 128), jnp.int32),
                 pltpu.SemaphoreType.DMA((4,)),
                 pltpu.SemaphoreType.DMA((N_MSG,)),
                 pltpu.SemaphoreType.DMA((N_MSG,)),
@@ -465,15 +518,15 @@
                 jax.ShapeDtypeStruct((3, 128, 256), F32),
                 jax.ShapeDtypeStruct((3, 128, 128), F32),
             ),
-            in_specs=[smem] * 3 + [vmem] * 5,
+            in_specs=[smem] * 3 + [vmem] * 7,
             out_specs=(vmem,) * 3,
             scratch_shapes=[
-                buf(3, ROWS, 128), buf(4, 3, 144, 128), buf(3, 96, 128), buf(3, 96, 128),
+                buf(4, 3, 144, 128), buf(3, 96, 128), buf(3, 96, 128),
                 buf(2, 3, 96, 128), buf(2, 3, 96, 128),
                 buf(3, 96, 128), buf(3, 96, 128), buf(3, 96, 128), buf(3, 96, 128),
             ],
             compiler_params=pltpu.CompilerParams(vmem_limit_bytes=24 << 20),
-        )(cnt, pos, ext, st, lslab, ulslab, dlc, err)
+        )(cnt, pos, ext, *parts, err)
 
     return jax.shard_map(
         per_device,

time: 26.7 us -> 25.7 us (0.963)
  the two profiles are of different devices: /device:TPU:1 before, /device:TPU:32 now
where the time goes in v3:
time: 25.7 us; the launch traced here: 25.6 us
  Pallas kernels  23.7 us (92%)
  between operations  1.93 us (8%)
    pallas_call x1, Pallas kernels, per_device(): pl.pallas_call(functools.partial(exchange_kernel, n_row, n_col), out_shap...  21.1 us
    pallas_call x1, Pallas kernels, per_device(): pl.pallas_call(patch_kernel, out_shape=(jax.ShapeDtypeStruct((64, 128), F...  2.57 us

profile of v3, /device:TPU:32, one launch (start us, length us, event | category | flops | bytes accessed | tf_op | source)
XLA Modules:
  0.0 25.6 jit_solution(11292029082301884095)
XLA Ops:
  1.9 21.1 %shard_map.76 = (f32[3,3,208,128]{3,2,1,0:T(8,128)S(1)}, f32[3,2,64,128]{3,2,1,0:T(8,128)S(1)}, f32[3,32,128]{2,1,0:T(8,128)S(1)}, f32[3,32,128]{2,1,0:T(8,128)S...) custom-call(f32[3,128,256]{2,1,0:T(8,128)} %state.1, ...), custom_call_target="tpu_custom_call" | custom-call | tf_op jit(solution)/shard_map/pallas_call | solution.py:490
  23.0 2.6 %shard_map.77 = (f32[64,128]{1,0:T(8,128)}, f32[3,128,256]{2,1,0:T(8,128)}, f32[3,128,128]{2,1,0:T(8,128)}) custom-call(s32[7,1,128]{2,1,0:T(1,128)S(4)} %get-tuple-element.13.cnt, s32[1,1,2]{2,1,0:T(1,128)S(4)} %get-tuple-element.14.pos, s32[1,1,2]{2,1,0:T(1,128)S(4)} %get-tuple-element.15.ext, f32[3,3,208,128]{3,2,1,0:T(8,128)S(1)} %get-tuple-element.16.st, ...), custom_call_target="tpu_custom_call" | custom-call | tf_op jit(solution)/shard_map/pallas_call | solution.py:514

commit v4 on v3

--- a/solution.py
+++ b/solution.py
@@ -53,13 +53,17 @@
     return jnp.where(a * b > 0, chosen, 0.0)
 
 
-def from_lower(xs, lane):
-    rolled = [roll(x, 1) for x in xs]
+def from_lower(xs, lane, hop=1):
+    rolled = [roll(x, hop) for x in xs]
+    if len(xs) == 1:
+        return rolled
     return [jnp.where(lane == 0, rolled[g - 1], rolled[g]) for g in range(len(xs))]
 
 
-def from_upper(xs, lane):
-    rolled = [roll(x, 127) for x in xs]
+def from_upper(xs, lane, hop=1):
+    rolled = [roll(x, -hop) for x in xs]
+    if len(xs) == 1:
+        return rolled
     return [
         jnp.where(lane == 127, rolled[(g + 1) % len(xs)], rolled[g])
         for g in range(len(xs))
@@ -74,7 +78,7 @@
                 vel[k, g, at, :] = value
 
 
-def step_pass(src, vel, dst, groups, first, last):
+def step_pass(src, vel, dst, groups, first, last, hop=1):
     lane = lanes()
     for i in range(first, last):
         row = 8 * i
@@ -88,12 +92,12 @@
             )
 
         along = [load(0, g, 2) for g in groups]
-        shifted = [from_lower([a[0][k] for a in along], lane) for k in range(3)]
+        shifted = [from_lower([a[0][k] for a in along], lane, hop) for k in range(3)]
         low = []
         for n in range(len(groups)):
             u = [x[n] for x in shifted]
             low.append(face(side(u, speeds(*u), 2), along[n]))
-        high = [from_upper([f[c] for f in low], lane) for c in range(3)]
+        high = [from_upper([f[c] for f in low], lane, hop) for c in range(3)]
         for n, g in enumerate(groups):
             here = load(0, g, 1)
             down = face(load(-1, g, 1), here)
@@ -103,17 +107,21 @@
                 dst[c, g, chunk(row), :] = here[0][c] - HALF * change
 
 
-def coarse_rows(src, row, g, c, even):
+def block_means(src, row, g, c):
     pair = src[c, g, pl.ds(row, 8, stride=2), :] + src[c, g, pl.ds(row + 1, 8, stride=2), :]
-    pair = pair + roll(pair, 127)
-    return 0.25 * jnp.take_along_axis(pair, even, axis=1, mode="promise_in_bounds")
+    return 0.25 * (pair + roll(pair, 127))
+
+
+def pick(x, index):
+    return jnp.take_along_axis(x, index, axis=1, mode="promise_in_bounds")
 
 
 def exchange_kernel(
     n_row, n_col, state, row_count, col_count, pos_hbm, ext_hbm,
     st, rm, l_low, l_high, ulc, dlc, drc, counts, pos, ext, err,
-    rpack, lpack, low_s, high_s, cnt_s, lr, rl, url, up_low, ahead,
+    rpack, lpack, low_s, high_s, cnt_s, lr, rl, url, up_low, ahead, sides,
     vel, rim, fine1, fine2, cgrid, cvel, cone,
+    strip, svel, strip1, svel1, strip2, sgrid, sgvel, sone,
     cnt, local_sem, send_sem, recv_sem,
 ):
     me_r, me_c = lax.axis_index("row"), lax.axis_index("col")
@@ -198,6 +206,15 @@
     for copy in copies[:17]:
         copy.start()
 
+    for c in range(3):
+        tile = None
+        for g, from_lane in ((0, 0), (1, 124)):
+            for k in range(16):
+                to = 64 * g + 4 * k
+                x = roll(st[c, g, chunk(BASE + 8 * k), :], to - from_lane)
+                tile = x if tile is None else jnp.where(lane >= to, x, tile)
+        sides[c] = tile
+
     even = lax.rem(2 * lane, 128)
     own = (0, 1)
     speed_pass(st, vel, own, 8, 24)
@@ -226,14 +243,14 @@
 
     def coarse_own(i):
         for c in range(3):
-            halves = [coarse_rows(st, BASE - 16 + 16 * i, g, c, even) for g in range(2)]
+            halves = [pick(block_means(st, BASE - 16 + 16 * i, g, c), even) for g in range(2)]
             cgrid[c, 0, chunk(8 * i), :] = jnp.where(lane < 64, *halves)
         speed_pass(cgrid, cvel, (0,), i, i + 1)
 
     def estimate(i):
         total = None
         for c in range(3):
-            halves = [coarse_rows(fine2, BASE + 16 * i, g, c, even) for g in range(2)]
+            halves = [pick(block_means(fine2, BASE + 16 * i, g, c), even) for g in range(2)]
             gap = jnp.abs(jnp.where(lane < 64, *halves) - cone[c, 0, chunk(8 * i + 8), :])
             total = gap if total is None else total + gap
         err[chunk(8 * i), :] = 10.0 * total
@@ -264,37 +281,58 @@
     estimate(7)
 
     left, right, corner = lr[...], rl[...], url[...]
+    part, place = lax.shift_right_logical(lane, 4), lax.bitwise_and(lane, 15)
+
+    def folded(a, b, c, d):
+        return jnp.where(place < 2, a, jnp.where(place < 8, b, jnp.where(place < 12, c, d)))
+
+    for j in range(4):
+        block = 2 * part + (j - 1)
+        own_at = lax.bitwise_and(4 * block + jnp.where(place < 8, place - 2, place + 56), 127)
+        for c in range(3):
+            at = lax.bitwise_and(32 * c + 2 * block + lax.bitwise_and(place, 1), 127)
+            own_cells = pick(sides[c], own_at)
+            x = folded(pick(left, at), own_cells, own_cells, pick(right, at))
+            if j == 0:
+                rows = chunk(BASE - 8)
+                above = folded(
+                    roll(ulc[c], 2), roll(st[c, 0, rows, :], 2),
+                    roll(st[c, 1, rows, :], 12), roll(corner, -18 - 32 * c),
+                )
+                x = jnp.where(part == 0, above, x)
+            if j == 3:
+                rows = chunk(BASE + 128)
+                below = folded(
+                    roll(dlc[c], -14), roll(st[c, 0, rows, :], 114),
+                    roll(st[c, 1, rows, :], -4), roll(drc[c], 124),
+                )
+                x = jnp.where(part == 7, below, x)
+            strip[c, 0, chunk(8 + 8 * j), :] = x
+    one = (0,)
+    speed_pass(strip, svel, one, 1, 5)
+    step_pass(strip, svel, strip1, one, 1, 5)
+    speed_pass(strip1, svel1, one, 1, 5)
+    step_pass(strip1, svel1, strip2, one, 2, 4)
+    for i in range(3):
+        for c in range(3):
+            sgrid[c, 0, chunk(8 * i), :] = block_means(strip, 16 * i, 0, c)
+    speed_pass(sgrid, sgvel, one, 0, 3)
+    step_pass(sgrid, sgvel, sone, one, 1, 2, 2)
+    total = None
+    for c in range(3):
+        gap = jnp.abs(block_means(strip2, 16, 0, c) - sone[c, 0, chunk(8), :])
+        total = gap if total is None else total + gap
+    total = 10.0 * total
+    for i in range(8):
+        at = chunk(8 * i)
+        value = jnp.where(lane == 127, roll(total, 117 - 16 * i), err[at, :])
+        err[at, :] = jnp.where(lane == 0, roll(total, -(16 * i + 2)), value)
+
     for c in range(3):
         for k in range(-8, 17):
-            at = chunk(BASE + 8 * k)
             col = 32 * c + 2 * k
-            r = roll(corner, -(col + 32)) if k < 0 else drc[c] if k == 16 else roll(right, -col)
-            if k >= -1:
-                ends = ulc[c] if k < 0 else dlc[c]
-                x = roll(left, 62 - col) if 0 <= k < 16 else roll(ends, 64)
-                x = jnp.where(lane < 64, x, roll(st[c, 0, at, :], 64))
-                r = jnp.where(lane < 32, r, jnp.where(lane < 124, x, st[c, 1, at, :]))
-            st[c, 2, at, :] = r
-    strip = (2,)
-    speed_pass(st, vel, strip, 7, 25)
-    step_pass(st, vel, fine1, strip, 7, 25)
-    speed_pass(fine1, vel, strip, 7, 25)
-    step_pass(fine1, vel, fine2, strip, 8, 24)
-    for i in range(10):
-        for c in range(3):
-            cgrid[c, 1, chunk(8 * i), :] = coarse_rows(st, BASE - 16 + 16 * i, 2, c, even)
-    speed_pass(cgrid, cvel, (1,), 0, 10)
-    step_pass(cgrid, cvel, cone, (1,), 1, 9)
-    for i in range(8):
-        total = None
-        for c in range(3):
-            fine = coarse_rows(fine2, BASE + 16 * i, 2, c, even)
-            gap = jnp.abs(fine - cone[c, 1, chunk(8 * i + 8), :])
-            total = gap if total is None else total + gap
-        total = 10.0 * total
-        at = chunk(8 * i)
-        value = jnp.where(lane == 127, total, err[at, :])
-        err[at, :] = jnp.where(lane == 0, roll(total, 96), value)
+            x = roll(corner, -(col + 32)) if k < 0 else drc[c] if k == 16 else roll(right, -col)
+            st[c, 2, chunk(BASE + 8 * k), :] = x
 
     for copy in copies[9:17]:
         copy.wait_recv()
@@ -385,7 +423,6 @@
         for c, value in enumerate(speeds(*u)):
             wvel[c, chunk(8 * k + 8), :] = value
 
-    front = lane < 64
     for k in range(10):
         row = 8 * k + 8
 
@@ -396,81 +433,78 @@
         here = load(0, 1)
         down, up = face(load(-1, 1), here), face(here, load(1, 1))
         across = load(0, 2)
-        lower = (
-            [roll(x, 1) for x in across[0]],
-            [roll(x, 1) for x in across[1]],
-            roll(across[2], 1),
-        )
-        left = face(lower, across)
+        lower = [roll(x, 1) for x in across[0]]
+        left = face(side(lower, speeds(*lower), 2), across)
         right = [roll(x, 127) for x in left]
         for a in range(2):
-            far = []
+            near = [[] for _ in range(4)]
             for c in range(3):
                 twice = 2.0 * here[1][c]
                 tall = up[c] - twice if a else twice - down[c]
-                mid_c = here[0][c] - HALF * tall
+                half_way = here[0][c] - HALF * tall
                 twice = 2.0 * across[1][c]
-                e = mid_c - HALF * (twice - left[c])
-                o = mid_c - HALF * (right[c] - twice)
-                center = jnp.where(front, roll(e, -2), roll(o, 62))
-                ctr[a, c, chunk(row), :] = center
+                e = half_way - HALF * (twice - left[c])
+                o = half_way - HALF * (right[c] - twice)
+                ctr[2 * a, c, chunk(row), :] = e
+                ctr[2 * a + 1, c, chunk(row), :] = o
                 if 1 <= k < 9:
-                    e62, o2 = roll(e, 62), roll(o, -1)
-                    l1 = jnp.where(front, o2, e62)
-                    r1 = jnp.where(front, roll(o, -2), roll(e, 61))
-                    l2 = jnp.where(front, roll(e, -1), roll(o, 63))
-                    r2 = jnp.where(front, roll(e, -3), roll(o, 61))
-                    d1, d2, d3, d4 = l1 - l2, center - l1, r1 - center, r2 - r1
-                    s_l, s_c, s_r = minmod(d1, d2), minmod(d2, d3), minmod(d3, d4)
-                    far.append(
-                        (l1 + 0.5 * s_l, center - 0.5 * s_c, center + 0.5 * s_c, r1 - 0.5 * s_r)
-                    )
+                    inner, outer = o - e, e - roll(o, 1)
+                    s_e, s_o = 0.5 * minmod(outer, inner), 0.5 * minmod(inner, roll(outer, 127))
+                    for i, x in enumerate((roll(o + s_o, 1), e - s_e, e + s_e, o - s_o)):
+                        near[i].append(x)
             if 1 <= k < 9:
-                sides = [[far[c][i] for c in range(3)] for i in range(4)]
-                sides = [side(s, speeds(*s), 2) for s in sides]
-                f_low, f_high = face(sides[0], sides[1]), face(sides[2], sides[3])
+                sides = [side(u, speeds(*u), 2) for u in near]
+                f_out, f_in = face(sides[0], sides[1]), face(sides[2], sides[3])
                 for c in range(3):
-                    dcol[a, c, chunk(row), :] = f_high[c] - f_low[c]
+                    dcol[2 * a, c, chunk(row), :] = f_in[c] - f_out[c]
+                    dcol[2 * a + 1, c, chunk(row), :] = roll(f_out[c], 127) - f_in[c]
 
     for k in range(10):
         row = 8 * k + 8
         at = chunk(row)
-        l_side, r_side = [], []
-        for c in range(3):
-            c0, c1 = ctr[0, c, at, :], ctr[1, c, at, :]
-            inner = c1 - c0
-            before = c0 - ctr[1, c, chunk(row - 1), :]
-            after = ctr[0, c, chunk(row + 1), :] - c1
-            s0, s1 = minmod(before, inner), minmod(inner, after)
-            base[c, at, :] = c0 - 0.5 * s0
-            plus[c, at, :] = c1 + 0.5 * s1
-            l_side.append(c0 + 0.5 * s0)
-            r_side.append(c1 - 0.5 * s1)
-        if 1 <= k < 9:
+        for b in range(2):
+            l_side, r_side = [], []
+            for c in range(3):
+                c0, c1 = ctr[b, c, at, :], ctr[2 + b, c, at, :]
+                inner = c1 - c0
+                before = c0 - ctr[2 + b, c, chunk(row - 1), :]
+                after = ctr[b, c, chunk(row + 1), :] - c1
+                s0, s1 = 0.5 * minmod(before, inner), 0.5 * minmod(inner, after)
+                base[b, c, at, :] = c0 - s0
+                plus[b, c, at, :] = c1 + s1
+                l_side.append(c0 + s0)
+                r_side.append(c1 - s1)
+            if 1 <= k < 9:
+                f = face(side(l_side, speeds(*l_side), 1), side(r_side, speeds(*r_side), 1))
+                for c in range(3):
+                    mid[b, c, at, :] = f[c]
+    for k in range(1, 10):
+        row = 8 * k + 8
+        for b in range(2):
+            l_side = [plus[b, c, chunk(row - 1), :] for c in range(3)]
+            r_side = [base[b, c, chunk(row), :] for c in range(3)]
             f = face(side(l_side, speeds(*l_side), 1), side(r_side, speeds(*r_side), 1))
             for c in range(3):
-                mid[c, at, :] = f[c]
-    for k in range(1, 10):
-        row = 8 * k + 8
-        l_side = [plus[c, chunk(row - 1), :] for c in range(3)]
-        r_side = [base[c, chunk(row), :] for c in range(3)]
-        f = face(side(l_side, speeds(*l_side), 1), side(r_side, speeds(*r_side), 1))
-        for c in range(3):
-            low[c, chunk(row), :] = f[c]
-    spread = lax.shift_right_logical(lane, 1) + 64 * lax.bitwise_and(lane, 1)
-    inside_col = lax.bitwise_and(lane, 63) < ext[0, 0, 1]
+                low[b, c, chunk(row), :] = f[c]
+    source = lax.shift_right_logical(lane, 1)
+    odd = lax.bitwise_and(lane, 1) == 1
+    inside_col = source < ext[0, 0, 1]
     for k in range(1, 9):
         row = 8 * k + 8
+        at = chunk(row)
         inside = inside_col & (row8 + 8 * (k - 1) < ext[0, 0, 0])
         for c in range(3):
-            at = chunk(row)
-            f_mid, f_low, f_next = mid[c, at, :], low[c, at, :], low[c, chunk(row + 1), :]
-            for a, tall in enumerate((f_mid - f_low, f_next - f_mid)):
-                done = ctr[a, c, at, :] - HALF * (tall + dcol[a, c, at, :])
-                done = jnp.where(inside, done, 0.0)
-                refined[c, pl.ds(16 * (k - 1) + a, 8, stride=2), :] = jnp.take_along_axis(
-                    done, spread, axis=1, mode="promise_in_bounds"
-                )
+            done = [[], []]
+            for b in range(2):
+                f_mid, f_low, f_next = mid[b, c, at, :], low[b, c, at, :], low[b, c, chunk(row + 1), :]
+                for a, tall in enumerate((f_mid - f_low, f_next - f_mid)):
+                    x = ctr[2 * a + b, c, at, :] - HALF * (tall + dcol[2 * a + b, c, at, :])
+                    done[a].append(
+                        pick(x, source + 2)
+                    )
+            for a in range(2):
+                x = jnp.where(odd, done[a][1], done[a][0])
+                refined[c, pl.ds(16 * (k - 1) + a, 8, stride=2), :] = jnp.where(inside, x, 0.0)
 
 
 def solution(mesh):
@@ -500,8 +534,9 @@
             out_specs=(vmem,) * 7 + (smem,) * 3 + (vmem,),
             scratch_shapes=[
                 buf(8, 128), buf(8, 128), half, half, pltpu.VMEM((1, 128), jnp.int32),
-                buf(8, 128), buf(8, 128), buf(8, 128), half, buf(3, 128, 128),
-                *([buf(3, 3, ROWS, 128)] * 4), *([buf(3, 2, 88, 128)] * 3),
+                buf(8, 128), buf(8, 128), buf(8, 128), half, buf(3, 128, 128), corner,
+                *([buf(3, 2, ROWS, 128)] * 4), *([buf(3, 1, 88, 128)] * 3),
+                *([buf(3, 1, 48, 128)] * 8),
                 pltpu.VMEM((6, 1, 128), jnp.int32),
                 pltpu.SemaphoreType.DMA((4,)),
                 pltpu.SemaphoreType.DMA((N_MSG,)),
@@ -522,8 +557,7 @@
             out_specs=(vmem,) * 3,
             scratch_shapes=[
                 buf(4, 3, 144, 128), buf(3, 96, 128), buf(3, 96, 128),
-                buf(2, 3, 96, 128), buf(2, 3, 96, 128),
-                buf(3, 96, 128), buf(3, 96, 128), buf(3, 96, 128), buf(3, 96, 128),
+                buf(4, 3, 96, 128), buf(4, 3, 96, 128), *([buf(2, 3, 96, 128)] * 4),
             ],
             compiler_params=pltpu.CompilerParams(vmem_limit_bytes=24 << 20),
         )(cnt, pos, ext, *parts, err)

time: 25.7 us -> 23.9 us (0.930)
  the two profiles are of different devices: /device:TPU:32 before, /device:TPU:25 now
where the time goes in v4:
time: 23.9 us; the launch traced here: 23.8 us
  Pallas kernels  21.8 us (91%)
  between operations  1.93 us (8%)
    pallas_call x1, Pallas kernels, per_device(): pl.pallas_call(functools.partial(exchange_kernel, n_row, n_col), out_shap...  19.5 us
    pallas_call x1, Pallas kernels, per_device(): pl.pallas_call(patch_kernel, out_shape=(jax.ShapeDtypeStruct((64, 128), F...  2.33 us

profile of v4, /device:TPU:25, one launch (start us, length us, event | category | flops | bytes accessed | tf_op | source)
XLA Modules:
  0.0 23.8 jit_solution(8740675786247369483)
XLA Ops:
  1.9 19.5 %shard_map.76 = (f32[3,3,208,128]{3,2,1,0:T(8,128)S(1)}, f32[3,2,64,128]{3,2,1,0:T(8,128)S(1)}, f32[3,32,128]{2,1,0:T(8,128)S(1)}, f32[3,32,128]{2,1,0:T(8,128)S...) custom-call(f32[3,128,256]{2,1,0:T(8,128)} %state.1, ...), custom_call_target="tpu_custom_call" | custom-call | tf_op jit(solution)/shard_map/pallas_call | solution.py:524
  21.4 2.3 %shard_map.77 = (f32[64,128]{1,0:T(8,128)}, f32[3,128,256]{2,1,0:T(8,128)}, f32[3,128,128]{2,1,0:T(8,128)}) custom-call(s32[7,1,128]{2,1,0:T(1,128)S(4)} %get-tuple-element.13.cnt, s32[1,1,2]{2,1,0:T(1,128)S(4)} %get-tuple-element.14.pos, s32[1,1,2]{2,1,0:T(1,128)S(4)} %get-tuple-element.15.ext, f32[3,3,208,128]{3,2,1,0:T(8,128)S(1)} %get-tuple-element.16.st, ...), custom_call_target="tpu_custom_call" | custom-call | tf_op jit(solution)/shard_map/pallas_call | solution.py:549

commit v5 on v4

--- a/solution.py
+++ b/solution.py
@@ -12,7 +12,7 @@
 HALF = 0.05
 BASE = 64
 ROWS = 208
-N_MSG = 18
+N_MSG = 13
 
 
 def chunk(start, size=8):
@@ -118,11 +118,11 @@
 
 def exchange_kernel(
     n_row, n_col, state, row_count, col_count, pos_hbm, ext_hbm,
-    st, rm, l_low, l_high, ulc, dlc, drc, counts, pos, ext, err,
-    rpack, lpack, low_s, high_s, cnt_s, lr, rl, url, up_low, ahead, sides,
+    st, rm, l_low, l_high, ulc, dl, counts, pos, ext, err,
+    rpack, lpack, low_s, high_s, dtile, cnt, lr, rl, url, dr, dn, up_low, ahead, sides,
     vel, rim, fine1, fine2, cgrid, cvel, cone,
     strip, svel, strip1, svel1, strip2, sgrid, sgvel, sone,
-    cnt, local_sem, send_sem, recv_sem,
+    local_sem, send_sem, recv_sem,
 ):
     me_r, me_c = lax.axis_index("row"), lax.axis_index("col")
 
@@ -149,7 +149,7 @@
     lane = lanes()
     row8 = lax.broadcasted_iota(jnp.int32, (8, 128), 0)
     rc = row_count[0, 0]
-    cnt_s[...] = jnp.where(lanes((1, 128)) == 0, rc, col_count[0, 0])
+    both_counts = jnp.where(lane == 96, rc, col_count[0, 0]).astype(F32)
     for load in loads:
         load.wait()
 
@@ -160,7 +160,7 @@
                 to = 32 * c + 2 * k
                 x = roll(columns(c, k), to - lane_at)
                 tile = x if tile is None else jnp.where(lane >= to, x, tile)
-        return tile
+        return jnp.where(lane >= 96, both_counts, tile)
 
     def fold(low, high):
         return jnp.where(lane < 64, roll(high, 64), low)
@@ -169,31 +169,29 @@
     lpack[...] = edge(lambda c, k: st[c, 0, chunk(BASE + 8 * k), :], 0)
     for c in range(3):
         for k in range(4):
-            low_s[c, chunk(8 * k), :] = fold(
+            low_s[chunk(32 * c + 8 * k), :] = fold(
                 st[c, 1, chunk(BASE + 64 + 8 * k), :], st[c, 1, chunk(BASE + 96 + 8 * k), :]
             )
 
+        dtile[pl.ds(2 * c, 2), :] = st[c, 1, pl.ds(BASE, 2), :]
+    low_s[chunk(96), :] = both_counts
+    dtile[pl.ds(6, 2), :] = both_counts[:2]
+
     pl.semaphore_wait(barrier, 8)
     both = pl.ds(0, 2)
-    head, tail = pl.ds(0, 2), pl.ds(6, 2)
     messages = [
         ((1, 0), low_s, up_low),
         ((0, 1), rpack, lr),
         ((0, -1), lpack, rl),
         ((1, 0), st.at[:, both, pl.ds(BASE + 112, 16), :], st.at[:, both, pl.ds(BASE - 16, 16), :]),
         ((-1, 0), st.at[:, both, pl.ds(BASE, 8), :], st.at[:, both, pl.ds(BASE + 128, 8), :]),
-        ((1, 1), st.at[:, 1, pl.ds(BASE + 126, 2), :], ulc.at[:, tail, :]),
+        ((1, 1), st.at[:, 1, pl.ds(BASE + 126, 2), :], ulc.at[:, pl.ds(6, 2), :]),
         ((1, -1), lpack, url),
-        ((-1, 1), st.at[:, 1, pl.ds(BASE, 2), :], dlc.at[:, head, :]),
-        ((-1, -1), st.at[:, 0, pl.ds(BASE, 2), :], drc.at[:, head, :]),
+        ((-1, 1), dtile, dl.at[chunk(0), :]),
+        ((-1, -1), lpack, dr),
+        ((-1, 0), lpack, dn),
         ((0, 1), low_s, l_low),
         ((1, 0), st.at[:, both, pl.ds(BASE + 64, 48), :], st.at[:, both, pl.ds(0, 48), :]),
-        ((0, -1), cnt_s, cnt.at[0]),
-        ((1, 0), cnt_s, cnt.at[1]),
-        ((-1, 0), cnt_s, cnt.at[2]),
-        ((1, -1), cnt_s, cnt.at[3]),
-        ((-1, 1), cnt_s, cnt.at[4]),
-        ((-1, -1), cnt_s, cnt.at[5]),
         ((0, 1), high_s, l_high),
     ]
     copies = [
@@ -203,7 +201,7 @@
         )
         for i, (to, src, dst) in enumerate(messages)
     ]
-    for copy in copies[:17]:
+    for copy in copies[:12]:
         copy.start()
 
     for c in range(3):
@@ -223,7 +221,7 @@
     copies[0].wait_recv()
     for c in range(3):
         for k in range(4):
-            x = up_low[c, chunk(8 * k), :]
+            x = up_low[chunk(32 * c + 8 * k), :]
             ahead[c, chunk(8 * k), :] = x
             ahead[c, chunk(32 + 8 * k), :] = roll(x, 64)
         for k in range(8):
@@ -239,7 +237,7 @@
         ]
         for k in range(4):
             high_s[c, chunk(8 * k), :] = fold(top[k], top[k + 4])
-    copies[17].start()
+    copies[12].start()
 
     def coarse_own(i):
         for c in range(3):
@@ -280,7 +278,7 @@
     estimate(0)
     estimate(7)
 
-    left, right, corner = lr[...], rl[...], url[...]
+    left, right, corner, lower_right = lr[...], rl[...], url[...], dr[...]
     part, place = lax.shift_right_logical(lane, 4), lax.bitwise_and(lane, 15)
 
     def folded(a, b, c, d):
@@ -303,8 +301,8 @@
             if j == 3:
                 rows = chunk(BASE + 128)
                 below = folded(
-                    roll(dlc[c], -14), roll(st[c, 0, rows, :], 114),
-                    roll(st[c, 1, rows, :], -4), roll(drc[c], 124),
+                    roll(dl[chunk(2 * c), :], -14), roll(st[c, 0, rows, :], 114),
+                    roll(st[c, 1, rows, :], -4), roll(lower_right, 124 - 32 * c),
                 )
                 x = jnp.where(part == 7, below, x)
             strip[c, 0, chunk(8 + 8 * j), :] = x
@@ -331,10 +329,13 @@
     for c in range(3):
         for k in range(-8, 17):
             col = 32 * c + 2 * k
-            x = roll(corner, -(col + 32)) if k < 0 else drc[c] if k == 16 else roll(right, -col)
+            if k < 0:
+                x = roll(corner, -(col + 32))
+            else:
+                x = roll(lower_right, -32 * c) if k == 16 else roll(right, -col)
             st[c, 2, chunk(BASE + 8 * k), :] = x
 
-    for copy in copies[9:17]:
+    for copy in copies[9:12]:
         copy.wait_recv()
     for c in range(3):
         for g in range(2):
@@ -342,37 +343,34 @@
                 here = st[c, g, chunk(BASE + 8 * k), :]
                 above = st[c, g, chunk(BASE + 8 * k - rc), :]
                 rm[c, g, chunk(8 * k), :] = jnp.where(row8 + 8 * k < rc, above, here)
-    copies[17].wait_recv()
-    keep = [
-        pltpu.make_async_copy(cnt, counts.at[pl.ds(0, 6)], local_sem.at[0]),
-        pltpu.make_async_copy(cnt_s, counts.at[6], local_sem.at[1]),
-    ]
-    for copy in keep:
-        copy.start()
+    given = (rl[:1], up_low[pl.ds(96, 1)], dn[:1], url[:1], dl[pl.ds(6, 1)], dr[:1], lpack[:1])
+    for i, x in enumerate(given):
+        cnt[pl.ds(i, 1), :] = x
+    keep = pltpu.make_async_copy(cnt, counts, local_sem.at[0])
+    keep.start()
+    copies[12].wait_recv()
     for copy in copies:
         copy.wait_send()
-    for copy in keep:
-        copy.wait()
+    keep.wait()
 
 
 def patch_kernel(
-    cnt, pos, ext, st, rm, l_low, l_high, ulc, dlc, err_in,
+    cnt, pos, ext, st, rm, l_low, l_high, ulc, dl, err_in,
     err, moved, refined,
     tiles, win, wvel, ctr, dcol, plus, base, mid, low,
 ):
     lane = lanes()
     row8 = lax.broadcasted_iota(jnp.int32, (8, 128), 0)
     err[...] = err_in[...]
-    rc_of = lambda i: cnt[i, 0, 0]
-    cc_of = lambda i: cnt[i, 0, 1]
+    rc_of = lambda i: cnt[i, 96].astype(jnp.int32)
+    cc_of = lambda i: cnt[i, 97].astype(jnp.int32)
     rows_below = (rc_of(4), rc_of(2), rc_of(2), rc_of(5))
     cols_in = {"up": (cc_of(1), cc_of(3)), "own": (cc_of(6), cc_of(0)), "down": (cc_of(2), cc_of(5))}
 
     rc_right = rc_of(0)
     for c in range(3):
         for k in range(4):
-            for start, half in ((0, l_high), (64, l_low)):
-                x = half[c, chunk(8 * k), :]
+            for start, x in ((0, l_high[c, chunk(8 * k), :]), (64, l_low[chunk(32 * c + 8 * k), :])):
                 tiles[0, c, chunk(8 + start + 8 * k), :] = x
                 tiles[0, c, chunk(40 + start + 8 * k), :] = roll(x, 64)
         tiles[0, c, chunk(0), :] = ulc[c]
@@ -396,7 +394,7 @@
                     st[c, 1, chunk(BASE + 128 - rows_below[2]), :],
                     st[c, 2, chunk(BASE + 128 - rows_below[3]), :],
                 ]
-                below = [dlc[c], st[c, 0, at, :], st[c, 1, at, :], st[c, 2, at, :]]
+                below = [dl[chunk(2 * c), :], st[c, 0, at, :], st[c, 1, at, :], st[c, 2, at, :]]
                 values = [jnp.where(row8 < rows_below[g], above[g], below[g]) for g in range(4)]
                 tiles[0, c, chunk(136), :] = values[0]
             c0, c_right = cols_in["up" if k < 0 else "down" if k == 16 else "own"]
@@ -521,23 +519,22 @@
         ]
         corner = buf(3, 8, 128)
         half = buf(3, 32, 128)
-        *parts, _, cnt, pos, ext, err = pl.pallas_call(
+        *parts, cnt, pos, ext, err = pl.pallas_call(
             functools.partial(exchange_kernel, n_row, n_col),
             out_shape=(
-                buf(3, 3, ROWS, 128), buf(3, 2, 64, 128), half, half, *([corner] * 3),
-                pltpu.SMEM((7, 1, 128), jnp.int32),
+                buf(3, 3, ROWS, 128), buf(3, 2, 64, 128), buf(104, 128), half, corner, buf(16, 128),
+                pltpu.SMEM((8, 128), F32),
                 pltpu.SMEM((1, 1, 2), jnp.int32),
                 pltpu.SMEM((1, 1, 2), jnp.int32),
                 buf(64, 128),
             ),
             in_specs=[hbm, smem, smem, hbm, hbm],
-            out_specs=(vmem,) * 7 + (smem,) * 3 + (vmem,),
+            out_specs=(vmem,) * 6 + (smem,) * 3 + (vmem,),
             scratch_shapes=[
-                buf(8, 128), buf(8, 128), half, half, pltpu.VMEM((1, 128), jnp.int32),
-                buf(8, 128), buf(8, 128), buf(8, 128), half, buf(3, 128, 128), corner,
+                buf(8, 128), buf(8, 128), buf(104, 128), half, *([buf(8, 128)] * 7),
+                buf(104, 128), buf(3, 128, 128), corner,
                 *([buf(3, 2, ROWS, 128)] * 4), *([buf(3, 1, 88, 128)] * 3),
                 *([buf(3, 1, 48, 128)] * 8),
-                pltpu.VMEM((6, 1, 128), jnp.int32),
                 pltpu.SemaphoreType.DMA((4,)),
                 pltpu.SemaphoreType.DMA((N_MSG,)),
                 pltpu.SemaphoreType.DMA((N_MSG,)),

time: 23.9 us -> 22.8 us (0.954)
  Pallas kernels: 21.8 us -> 20.8 us
    pallas_call x1, Pallas kernels: 19.5 us -> 18.5 us  [per_device(): pl.pallas_call(functools.partial(exchange_kernel, n_row, n_col), out_shap...]
where the time goes in v5:
time: 22.8 us; the launch traced here: 22.7 us
  Pallas kernels  20.8 us (91%)
  between operations  1.93 us (8%)
    pallas_call x1, Pallas kernels, per_device(): pl.pallas_call(functools.partial(exchange_kernel, n_row, n_col), out_shap...  18.5 us
    pallas_call x1, Pallas kernels, per_device(): pl.pallas_call(patch_kernel, out_shape=(jax.ShapeDtypeStruct((64, 128), F...  2.33 us

profile of v5, /device:TPU:25, one launch (start us, length us, event | category | flops | bytes accessed | tf_op | source)
XLA Modules:
  0.0 22.7 jit_solution(16886037702782375751)
XLA Ops:
  1.9 18.5 %shard_map.76 = (f32[3,3,208,128]{3,2,1,0:T(8,128)S(1)}, f32[3,2,64,128]{3,2,1,0:T(8,128)S(1)}, f32[104,128]{1,0:T(8,128)S(1)}, f32[3,32,128]{2,1,0:T(8,128)S(1)...) custom-call(f32[3,128,256]{2,1,0:T(8,128)} %state.1, ...), custom_call_target="tpu_custom_call" | custom-call | tf_op jit(solution)/shard_map/pallas_call | solution.py:522
  20.4 2.3 %shard_map.77 = (f32[64,128]{1,0:T(8,128)}, f32[3,128,256]{2,1,0:T(8,128)}, f32[3,128,128]{2,1,0:T(8,128)}) custom-call(f32[8,128]{1,0:T(8,128)S(4)} %get-tuple-element.13.cnt, s32[1,1,2]{2,1,0:T(1,128)S(4)} %get-tuple-element.14.pos, s32[1,1,2]{2,1,0:T(1,128)S(4)} %get-tuple-element.15.ext, f32[3,3,208,128]{3,2,1,0:T(8,128)S(1)} %get-tuple-element.16.st, ...), custom_call_target="tpu_custom_call" | custom-call | tf_op jit(solution)/shard_map/pallas_call | solution.py:546

commit v6 on v5

--- a/solution.py
+++ b/solution.py
@@ -10,9 +10,9 @@
 MESH = pl.DeviceIdType.MESH
 F32 = jnp.float32
 HALF = 0.05
-BASE = 64
-ROWS = 208
-N_MSG = 13
+BASE = 80
+ROWS = 224
+N_MSG = 11
 
 
 def chunk(start, size=8):
@@ -107,8 +107,8 @@
                 dst[c, g, chunk(row), :] = here[0][c] - HALF * change
 
 
-def block_means(src, row, g, c):
-    pair = src[c, g, pl.ds(row, 8, stride=2), :] + src[c, g, pl.ds(row + 1, 8, stride=2), :]
+def block_means(src, row, g, c, n=8):
+    pair = src[c, g, pl.ds(row, n, stride=2), :] + src[c, g, pl.ds(row + 1, n, stride=2), :]
     return 0.25 * (pair + roll(pair, 127))
 
 
@@ -118,8 +118,8 @@
 
 def exchange_kernel(
     n_row, n_col, state, row_count, col_count, pos_hbm, ext_hbm,
-    st, rm, l_low, l_high, ulc, dl, counts, pos, ext, err,
-    rpack, lpack, low_s, high_s, dtile, cnt, lr, rl, url, dr, dn, up_low, ahead, sides,
+    st, rm, l_low, l_high, ul, dl, counts, pos, ext, err,
+    lpack, low_s, high_s, utile, cnt, rl, url, dr, dn, up_low, ahead, sides,
     vel, rim, fine1, fine2, cgrid, cvel, cone,
     strip, svel, strip1, svel1, strip2, sgrid, sgvel, sone,
     local_sem, send_sem, recv_sem,
@@ -165,7 +165,7 @@
     def fold(low, high):
         return jnp.where(lane < 64, roll(high, 64), low)
 
-    rpack[...] = edge(lambda c, k: st[c, 1, chunk(BASE + 8 * k), :], 126)
+    low_s[chunk(104), :] = edge(lambda c, k: st[c, 1, chunk(BASE + 8 * k), :], 126)
     lpack[...] = edge(lambda c, k: st[c, 0, chunk(BASE + 8 * k), :], 0)
     for c in range(3):
         for k in range(4):
@@ -173,25 +173,26 @@
                 st[c, 1, chunk(BASE + 64 + 8 * k), :], st[c, 1, chunk(BASE + 96 + 8 * k), :]
             )
 
-        dtile[pl.ds(2 * c, 2), :] = st[c, 1, pl.ds(BASE, 2), :]
+        for g in range(2):
+            utile[pl.ds(4 * c + 2 * g, 2), :] = st[c, g, pl.ds(BASE, 2), :]
+            low_s[pl.ds(112 + 4 * c + 2 * g, 2), :] = st[c, g, pl.ds(BASE + 126, 2), :]
     low_s[chunk(96), :] = both_counts
-    dtile[pl.ds(6, 2), :] = both_counts[:2]
+    low_s[pl.ds(124, 4), :] = both_counts[:4]
+    utile[pl.ds(12, 4), :] = both_counts[:4]
 
     pl.semaphore_wait(barrier, 8)
     both = pl.ds(0, 2)
     messages = [
         ((1, 0), low_s, up_low),
-        ((0, 1), rpack, lr),
+        ((0, 1), low_s.at[pl.ds(104, 8), :], l_low.at[pl.ds(104, 8), :]),
         ((0, -1), lpack, rl),
-        ((1, 0), st.at[:, both, pl.ds(BASE + 112, 16), :], st.at[:, both, pl.ds(BASE - 16, 16), :]),
-        ((-1, 0), st.at[:, both, pl.ds(BASE, 8), :], st.at[:, both, pl.ds(BASE + 128, 8), :]),
-        ((1, 1), st.at[:, 1, pl.ds(BASE + 126, 2), :], ulc.at[:, pl.ds(6, 2), :]),
+        ((-1, 0), utile, dn),
+        ((1, 1), low_s.at[pl.ds(112, 16), :], ul.at[pl.ds(8, 16), :]),
         ((1, -1), lpack, url),
-        ((-1, 1), dtile, dl.at[chunk(0), :]),
+        ((-1, 1), utile, dl.at[pl.ds(0, 16), :]),
         ((-1, -1), lpack, dr),
-        ((-1, 0), lpack, dn),
-        ((0, 1), low_s, l_low),
-        ((1, 0), st.at[:, both, pl.ds(BASE + 64, 48), :], st.at[:, both, pl.ds(0, 48), :]),
+        ((0, 1), low_s.at[pl.ds(0, 104), :], l_low.at[pl.ds(0, 104), :]),
+        ((1, 0), st.at[:, both, pl.ds(BASE + 64, 64), :], st.at[:, both, pl.ds(0, 64), :]),
         ((0, 1), high_s, l_high),
     ]
     copies = [
@@ -201,7 +202,7 @@
         )
         for i, (to, src, dst) in enumerate(messages)
     ]
-    for copy in copies[:12]:
+    for copy in copies[:9]:
         copy.start()
 
     for c in range(3):
@@ -215,8 +216,8 @@
 
     even = lax.rem(2 * lane, 128)
     own = (0, 1)
-    speed_pass(st, vel, own, 8, 24)
-    step_pass(st, vel, fine1, own, 9, 23)
+    speed_pass(st, vel, own, 10, 26)
+    step_pass(st, vel, fine1, own, 11, 25)
 
     copies[0].wait_recv()
     for c in range(3):
@@ -237,12 +238,15 @@
         ]
         for k in range(4):
             high_s[c, chunk(8 * k), :] = fold(top[k], top[k + 4])
-    copies[12].start()
+    copies[10].start()
+    copies[9].start()
 
     def coarse_own(i):
-        for c in range(3):
-            halves = [pick(block_means(st, BASE - 16 + 16 * i, g, c), even) for g in range(2)]
-            cgrid[c, 0, chunk(8 * i), :] = jnp.where(lane < 64, *halves)
+        n = 8 if i else 4
+        for c in range(3):
+            row = BASE - 2 * n + 16 * i
+            halves = [pick(block_means(st, row, g, c, n), even[:n]) for g in range(2)]
+            cgrid[c, 0, pl.ds(8 * i + 8 - n, n), :] = jnp.where(lane[:n] < 64, *halves)
         speed_pass(cgrid, cvel, (0,), i, i + 1)
 
     def estimate(i):
@@ -253,24 +257,28 @@
             total = gap if total is None else total + gap
         err[chunk(8 * i), :] = 10.0 * total
 
-    speed_pass(fine1, vel, own, 9, 23)
-    step_pass(fine1, vel, fine2, own, 10, 22)
+    speed_pass(fine1, vel, own, 11, 25)
+    step_pass(fine1, vel, fine2, own, 12, 24)
     for i in range(1, 9):
         coarse_own(i)
     step_pass(cgrid, cvel, cone, (0,), 2, 8)
     for i in range(1, 7):
         estimate(i)
 
-    for copy in copies[1:9]:
+    for copy in copies[1:8]:
         copy.wait_recv()
-    speed_pass(st, rim, own, 7, 10)
-    speed_pass(st, rim, own, 22, 25)
-    step_pass(st, rim, fine1, own, 7, 9)
-    step_pass(st, rim, fine1, own, 23, 25)
-    speed_pass(fine1, rim, own, 7, 11)
-    speed_pass(fine1, rim, own, 21, 25)
-    step_pass(fine1, rim, fine2, own, 8, 10)
-    step_pass(fine1, rim, fine2, own, 22, 24)
+    for c in range(3):
+        for g in range(2):
+            st[c, g, pl.ds(BASE - 2, 2), :] = up_low[pl.ds(112 + 4 * c + 2 * g, 2), :]
+            st[c, g, pl.ds(BASE + 128, 2), :] = dn[pl.ds(4 * c + 2 * g, 2), :]
+    speed_pass(st, rim, own, 9, 12)
+    speed_pass(st, rim, own, 24, 27)
+    step_pass(st, rim, fine1, own, 9, 11)
+    step_pass(st, rim, fine1, own, 25, 27)
+    speed_pass(fine1, rim, own, 9, 13)
+    speed_pass(fine1, rim, own, 23, 27)
+    step_pass(fine1, rim, fine2, own, 10, 12)
+    step_pass(fine1, rim, fine2, own, 24, 26)
     coarse_own(0)
     coarse_own(9)
     step_pass(cgrid, cvel, cone, (0,), 1, 2)
@@ -278,7 +286,7 @@
     estimate(0)
     estimate(7)
 
-    left, right, corner, lower_right = lr[...], rl[...], url[...], dr[...]
+    left, right, corner, lower_right = l_low[chunk(104), :], rl[...], url[...], dr[...]
     part, place = lax.shift_right_logical(lane, 4), lax.bitwise_and(lane, 15)
 
     def folded(a, b, c, d):
@@ -294,14 +302,14 @@
             if j == 0:
                 rows = chunk(BASE - 8)
                 above = folded(
-                    roll(ulc[c], 2), roll(st[c, 0, rows, :], 2),
+                    roll(ul[chunk(4 + 4 * c), :], 2), roll(st[c, 0, rows, :], 2),
                     roll(st[c, 1, rows, :], 12), roll(corner, -18 - 32 * c),
                 )
                 x = jnp.where(part == 0, above, x)
             if j == 3:
                 rows = chunk(BASE + 128)
                 below = folded(
-                    roll(dl[chunk(2 * c), :], -14), roll(st[c, 0, rows, :], 114),
+                    roll(dl[chunk(2 + 4 * c), :], -14), roll(st[c, 0, rows, :], 114),
                     roll(st[c, 1, rows, :], -4), roll(lower_right, 124 - 32 * c),
                 )
                 x = jnp.where(part == 7, below, x)
@@ -335,27 +343,27 @@
                 x = roll(lower_right, -32 * c) if k == 16 else roll(right, -col)
             st[c, 2, chunk(BASE + 8 * k), :] = x
 
-    for copy in copies[9:12]:
+    for copy in copies[8:10]:
         copy.wait_recv()
     for c in range(3):
         for g in range(2):
             for k in range(8):
                 here = st[c, g, chunk(BASE + 8 * k), :]
-                above = st[c, g, chunk(BASE + 8 * k - rc), :]
+                above = st[c, g, chunk(64 + 8 * k - rc), :]
                 rm[c, g, chunk(8 * k), :] = jnp.where(row8 + 8 * k < rc, above, here)
-    given = (rl[:1], up_low[pl.ds(96, 1)], dn[:1], url[:1], dl[pl.ds(6, 1)], dr[:1], lpack[:1])
+    given = (rl[:1], up_low[pl.ds(96, 1)], dn[pl.ds(12, 1)], url[:1], dl[pl.ds(12, 1)], dr[:1], lpack[:1])
     for i, x in enumerate(given):
         cnt[pl.ds(i, 1), :] = x
     keep = pltpu.make_async_copy(cnt, counts, local_sem.at[0])
     keep.start()
-    copies[12].wait_recv()
+    copies[10].wait_recv()
     for copy in copies:
         copy.wait_send()
     keep.wait()
 
 
 def patch_kernel(
-    cnt, pos, ext, st, rm, l_low, l_high, ulc, dl, err_in,
+    cnt, pos, ext, st, rm, l_low, l_high, ul, dl, err_in,
     err, moved, refined,
     tiles, win, wvel, ctr, dcol, plus, base, mid, low,
 ):
@@ -373,13 +381,13 @@
             for start, x in ((0, l_high[c, chunk(8 * k), :]), (64, l_low[chunk(32 * c + 8 * k), :])):
                 tiles[0, c, chunk(8 + start + 8 * k), :] = x
                 tiles[0, c, chunk(40 + start + 8 * k), :] = roll(x, 64)
-        tiles[0, c, chunk(0), :] = ulc[c]
+        tiles[0, c, chunk(0), :] = ul[chunk(4 + 4 * c), :]
 
     for c in range(3):
         for k in range(-1, 17):
             at = chunk(BASE + 8 * k)
             if k < 0:
-                values = [ulc[c], st[c, 0, at, :], st[c, 1, at, :], st[c, 2, at, :]]
+                values = [ul[chunk(4 + 4 * c), :], st[c, 0, at, :], st[c, 1, at, :], st[c, 2, at, :]]
             elif k < 16:
                 own = [rm[c, g, chunk(8 * k), :] if k < 8 else st[c, g, at, :] for g in range(2)]
                 beside = st[c, 2, at, :]
@@ -394,7 +402,7 @@
                     st[c, 1, chunk(BASE + 128 - rows_below[2]), :],
                     st[c, 2, chunk(BASE + 128 - rows_below[3]), :],
                 ]
-                below = [dl[chunk(2 * c), :], st[c, 0, at, :], st[c, 1, at, :], st[c, 2, at, :]]
+                below = [dl[chunk(2 + 4 * c), :], st[c, 0, at, :], st[c, 1, at, :], st[c, 2, at, :]]
                 values = [jnp.where(row8 < rows_below[g], above[g], below[g]) for g in range(4)]
                 tiles[0, c, chunk(136), :] = values[0]
             c0, c_right = cols_in["up" if k < 0 else "down" if k == 16 else "own"]
@@ -522,7 +530,7 @@
         *parts, cnt, pos, ext, err = pl.pallas_call(
             functools.partial(exchange_kernel, n_row, n_col),
             out_shape=(
-                buf(3, 3, ROWS, 128), buf(3, 2, 64, 128), buf(104, 128), half, corner, buf(16, 128),
+                buf(3, 3, ROWS, 128), buf(3, 2, 64, 128), buf(112, 128), half, buf(32, 128), buf(24, 128),
                 pltpu.SMEM((8, 128), F32),
                 pltpu.SMEM((1, 1, 2), jnp.int32),
                 pltpu.SMEM((1, 1, 2), jnp.int32),
@@ -531,8 +539,8 @@
             in_specs=[hbm, smem, smem, hbm, hbm],
             out_specs=(vmem,) * 6 + (smem,) * 3 + (vmem,),
             scratch_shapes=[
-                buf(8, 128), buf(8, 128), buf(104, 128), half, *([buf(8, 128)] * 7),
-                buf(104, 128), buf(3, 128, 128), corner,
+                buf(8, 128), buf(128, 128), half, buf(16, 128), *([buf(8, 128)] * 4), buf(16, 128),
+                buf(128, 128), buf(3, 128, 128), corner,
                 *([buf(3, 2, ROWS, 128)] * 4), *([buf(3, 1, 88, 128)] * 3),
                 *([buf(3, 1, 48, 128)] * 8),
                 pltpu.SemaphoreType.DMA((4,)),

time: 22.8 us -> 22.2 us (0.974)
  the two profiles are of different devices: /device:TPU:25 before, /device:TPU:1 now
where the time goes in v6:
time: 22.2 us; the launch traced here: 22 us
  Pallas kernels  20.1 us (91%)
  between operations  1.93 us (9%)
    pallas_call x1, Pallas kernels, per_device(): pl.pallas_call(functools.partial(exchange_kernel, n_row, n_col), out_shap...  17.8 us
    pallas_call x1, Pallas kernels, per_device(): pl.pallas_call(patch_kernel, out_shape=(jax.ShapeDtypeStruct((64, 128), F...  2.34 us

profile of v6, /device:TPU:1, one launch (start us, length us, event | category | flops | bytes accessed | tf_op | source)
XLA Modules:
  0.0 22.0 jit_solution(8749090710371716022)
XLA Ops:
  1.9 17.8 %shard_map.76 = (f32[3,3,224,128]{3,2,1,0:T(8,128)S(1)}, f32[3,2,64,128]{3,2,1,0:T(8,128)S(1)}, f32[112,128]{1,0:T(8,128)S(1)}, f32[3,32,128]{2,1,0:T(8,128)S(1)...) custom-call(f32[3,128,256]{2,1,0:T(8,128)} %state.1, ...), custom_call_target="tpu_custom_call" | custom-call | tf_op jit(solution)/shard_map/pallas_call | solution.py:530
  19.7 2.3 %shard_map.77 = (f32[64,128]{1,0:T(8,128)}, f32[3,128,256]{2,1,0:T(8,128)}, f32[3,128,128]{2,1,0:T(8,128)}) custom-call(f32[8,128]{1,0:T(8,128)S(4)} %get-tuple-element.13.cnt, s32[1,1,2]{2,1,0:T(1,128)S(4)} %get-tuple-element.14.pos, s32[1,1,2]{2,1,0:T(1,128)S(4)} %get-tuple-element.15.ext, f32[3,3,224,128]{3,2,1,0:T(8,128)S(1)} %get-tuple-element.16.st, ...), custom_call_target="tpu_custom_call" | custom-call | tf_op jit(solution)/shard_map/pallas_call | solution.py:554

commit v7 on v6

--- a/solution.py
+++ b/solution.py
@@ -139,18 +139,18 @@
         pltpu.make_async_copy(pos_hbm, pos, local_sem.at[2]),
         pltpu.make_async_copy(ext_hbm, ext, local_sem.at[3]),
     ]
-    for load in loads:
-        load.start()
     barrier = pltpu.get_barrier_semaphore()
     around = [(a, b) for a in (-1, 0, 1) for b in (-1, 0, 1) if (a, b) != (0, 0)]
     for a, b in around:
         pl.semaphore_signal(barrier, inc=1, device_id=device(a, b), device_id_type=MESH)
+    for load in loads[:2]:
+        load.start()
 
     lane = lanes()
     row8 = lax.broadcasted_iota(jnp.int32, (8, 128), 0)
     rc = row_count[0, 0]
     both_counts = jnp.where(lane == 96, rc, col_count[0, 0]).astype(F32)
-    for load in loads:
+    for load in loads[:2]:
         load.wait()
 
     def edge(columns, lane_at):
@@ -204,6 +204,8 @@
     ]
     for copy in copies[:9]:
         copy.start()
+    for load in loads[2:]:
+        load.start()
 
     for c in range(3):
         tile = None
@@ -267,6 +269,8 @@
 
     for copy in copies[1:8]:
         copy.wait_recv()
+    for load in loads[2:]:
+        load.wait()
     for c in range(3):
         for g in range(2):
             st[c, g, pl.ds(BASE - 2, 2), :] = up_low[pl.ds(112 + 4 * c + 2 * g, 2), :]
@@ -364,12 +368,16 @@
 
 def patch_kernel(
     cnt, pos, ext, st, rm, l_low, l_high, ul, dl, err_in,
-    err, moved, refined,
-    tiles, win, wvel, ctr, dcol, plus, base, mid, low,
+    err, moved_out, refined,
+    tiles, win, wvel, ctr, dcol, plus, base, mid, low, moved, sem,
 ):
     lane = lanes()
     row8 = lax.broadcasted_iota(jnp.int32, (8, 128), 0)
-    err[...] = err_in[...]
+    writes = [
+        pltpu.make_async_copy(err_in, err, sem.at[0]),
+        pltpu.make_async_copy(moved, moved_out, sem.at[1]),
+    ]
+    writes[0].start()
     rc_of = lambda i: cnt[i, 96].astype(jnp.int32)
     cc_of = lambda i: cnt[i, 97].astype(jnp.int32)
     rows_below = (rc_of(4), rc_of(2), rc_of(2), rc_of(5))
@@ -414,6 +422,8 @@
             if 0 <= k < 16:
                 moved[c, chunk(8 * k), pl.ds(0, 128)] = m0
                 moved[c, chunk(8 * k), pl.ds(128, 128)] = values[2]
+
+    writes[1].start()
 
     p0, p1 = pos[0, 0, 0], pos[0, 0, 1]
     group = lax.shift_right_logical(p1 + 126, 7)
@@ -511,6 +521,8 @@
             for a in range(2):
                 x = jnp.where(odd, done[a][1], done[a][0])
                 refined[c, pl.ds(16 * (k - 1) + a, 8, stride=2), :] = jnp.where(inside, x, 0.0)
+    for write in writes:
+        write.wait()
 
 
 def solution(mesh):
@@ -559,10 +571,11 @@
                 jax.ShapeDtypeStruct((3, 128, 128), F32),
             ),
             in_specs=[smem] * 3 + [vmem] * 7,
-            out_specs=(vmem,) * 3,
+            out_specs=(hbm, hbm, vmem),
             scratch_shapes=[
                 buf(4, 3, 144, 128), buf(3, 96, 128), buf(3, 96, 128),
                 buf(4, 3, 96, 128), buf(4, 3, 96, 128), *([buf(2, 3, 96, 128)] * 4),
+                buf(3, 128, 256), pltpu.SemaphoreType.DMA((2,)),
             ],
             compiler_params=pltpu.CompilerParams(vmem_limit_bytes=24 << 20),
         )(cnt, pos, ext, *parts, err)

time: 22.2 us -> 22.2 us (level)
  no operation moved by 1% of the time
where the time goes in v7:
time: 22.2 us; the launch traced here: 22 us
  Pallas kernels  20.1 us (91%)
  between operations  1.93 us (9%)
    pallas_call x1, Pallas kernels, per_device(): pl.pallas_call(functools.partial(exchange_kernel, n_row, n_col), out_shap...  17.8 us
    pallas_call x1, Pallas kernels, per_device(): pl.pallas_call(patch_kernel, out_shape=(jax.ShapeDtypeStruct((64, 128), F...  2.33 us

profile of v7, /device:TPU:1, one launch (start us, length us, event | category | flops | bytes accessed | tf_op | source)
XLA Modules:
  0.0 22.0 jit_solution(18441529727826725678)
XLA Ops:
  1.9 17.8 %shard_map.76 = (f32[3,3,224,128]{3,2,1,0:T(8,128)S(1)}, f32[3,2,64,128]{3,2,1,0:T(8,128)S(1)}, f32[112,128]{1,0:T(8,128)S(1)}, f32[3,32,128]{2,1,0:T(8,128)S(1)...) custom-call(f32[3,128,256]{2,1,0:T(8,128)} %state.1, ...), custom_call_target="tpu_custom_call" | custom-call | tf_op jit(solution)/shard_map/pallas_call | solution.py:542
  19.7 2.3 %shard_map.77 = (f32[64,128]{1,0:T(8,128)}, f32[3,128,256]{2,1,0:T(8,128)}, f32[3,128,128]{2,1,0:T(8,128)}) custom-call(f32[8,128]{1,0:T(8,128)S(4)} %get-tuple-element.13.cnt, s32[1,1,2]{2,1,0:T(1,128)S(4)} %get-tuple-element.14.pos, s32[1,1,2]{2,1,0:T(1,128)S(4)} %get-tuple-element.15.ext, f32[3,3,224,128]{3,2,1,0:T(8,128)S(1)} %get-tuple-element.16.st, ...), custom_call_target="tpu_custom_call" | custom-call | tf_op jit(solution)/shard_map/pallas_call | solution.py:566

commit v8 on v7

--- a/solution.py
+++ b/solution.py
@@ -28,7 +28,9 @@
 
 
 def speeds(h, m1, m2):
-    return m1 / h, m2 / h, jnp.sqrt(h)
+    r = lax.rsqrt(h)
+    inverse = r * r
+    return m1 * inverse, m2 * inverse, h * r
 
 
 def side(u, vel, normal):

time: 22.2 us -> 22.1 us (level)
  no operation moved by 1% of the time
where the time goes in v8:
time: 22.1 us; the launch traced here: 22 us
  Pallas kernels  20 us (90%)
  between operations  1.93 us (9%)
    pallas_call x1, Pallas kernels, per_device(): pl.pallas_call(functools.partial(exchange_kernel, n_row, n_col), out_shap...  17.8 us
    pallas_call x1, Pallas kernels, per_device(): pl.pallas_call(patch_kernel, out_shape=(jax.ShapeDtypeStruct((64, 128), F...  2.25 us

profile of v8, /device:TPU:1, one launch (start us, length us, event | category | flops | bytes accessed | tf_op | source)
XLA Modules:
  0.0 22.0 jit_solution(8983463627836138717)
XLA Ops:
  1.9 17.8 %shard_map.76 = (f32[3,3,224,128]{3,2,1,0:T(8,128)S(1)}, f32[3,2,64,128]{3,2,1,0:T(8,128)S(1)}, f32[112,128]{1,0:T(8,128)S(1)}, f32[3,32,128]{2,1,0:T(8,128)S(1)...) custom-call(f32[3,128,256]{2,1,0:T(8,128)} %state.1, ...), custom_call_target="tpu_custom_call" | custom-call | tf_op jit(solution)/shard_map/pallas_call | solution.py:544
  19.7 2.3 %shard_map.77 = (f32[64,128]{1,0:T(8,128)}, f32[3,128,256]{2,1,0:T(8,128)}, f32[3,128,128]{2,1,0:T(8,128)}) custom-call(f32[8,128]{1,0:T(8,128)S(4)} %get-tuple-element.13.cnt, s32[1,1,2]{2,1,0:T(1,128)S(4)} %get-tuple-element.14.pos, s32[1,1,2]{2,1,0:T(1,128)S(4)} %get-tuple-element.15.ext, f32[3,3,224,128]{3,2,1,0:T(8,128)S(1)} %get-tuple-element.16.st, ...), custom_call_target="tpu_custom_call" | custom-call | tf_op jit(solution)/shard_map/pallas_call | solution.py:568
